TPU v7x, 256 devices: a whole 4x4x8 slice. The times are simulated.
256 devices in a mesh: hist: 8 (over z), rows: 8 (over x_hi, y), dom: 4 (over x_lo, core).
Axes of the slice: x: 4 (x_hi: 2, x_lo: 2; x = x_hi * 2 + x_lo), y: 4, z: 8, core: 2. Of those that a mesh axis runs over, the one named last changes fastest.
Arguments:
- row_index: int32 [4, 262144], P(None, ('hist', 'rows', 'dom')), may hold values from 0 to 510
- col_index: int32 [4, 262144], P(None, ('hist', 'rows', 'dom')), may hold values from 0 to 510
- bin_index: int32 [4, 262144], P(None, ('hist', 'rows', 'dom')), may hold values from 0 to 255
- charge: bfloat16 [262144], P(('hist', 'rows', 'dom')), may hold values from 0.5 to 2
- momentum: float32 [2, 262144], P(None, ('hist', 'rows', 'dom')), may hold values from -6 to 6
- history: bfloat16 [64, 512, 512], P('hist', 'rows'), may hold values from 0 to 2
- kernel_cols: bfloat16 [64, 512, 512], P('hist', 'dom'), may hold values from -0.25 to 0.25
- kernel_rows: bfloat16 [64, 512, 2, 512], P('hist', 'rows'), may hold values from -0.03125 to 0.03125
Outputs:
- momentum_out: float32 [2, 262144], P(None, ('hist', 'rows', 'dom'))
- history_out: bfloat16 [64, 512, 512], P('hist', 'rows')
All inputs are finite; a program needn't handle non-finite values.
Results may differ from a plain program's by a relative error of at most 0.0024.
Values may be sent and summed in bfloat16 or wider, within the bound.
No kernel may reach another device: no remote copies, remote signals or barrier semaphores. Data moves between devices by JAX's collectives and lax.ppermute only.
A program may use at most 64 MiB of HBM per device.

v0:
```python
import jax
import jax.numpy as jnp
from jax import lax
from jax.sharding import PartitionSpec as P

NG = 512
BINS = 16
STEPS = 4


kick_scale = 0.5


def from_behind(array, axis, by):
    size = lax.axis_size(axis)
    pairs = [(i, i + by) for i in range(size) if 0 <= i + by < size]
    return lax.ppermute(array, axis, pairs)


def padded_to(lines, size):
    spare = -lines.shape[0] % size
    if not spare:
        return lines
    return jnp.concatenate([lines, jnp.zeros((spare, *lines.shape[1:]), lines.dtype)])


def in_order(blocks, dim):
    blocks = jnp.moveaxis(blocks, 0, dim)
    dims = blocks.shape
    return blocks.reshape(*dims[:dim], dims[dim] * dims[dim + 1], *dims[dim + 2 :])


def from_everyone(array, axis):
    copies = jnp.broadcast_to(array, (lax.axis_size(axis), *array.shape))
    return lax.all_to_all(copies, axis, split_axis=0, concat_axis=0, tiled=True)


def gather_directly(array, axis, dim):
    return in_order(from_everyone(array, axis), dim)


def split_up(array, dim, size):
    before, after = (array.shape[:dim], array.shape[dim + 1 :])
    return jnp.moveaxis(array.reshape(*before, size, -1, *after), dim, 0)


def sum_at_owner(array, axis, dim):
    size = lax.axis_size(axis)
    blocks = lax.all_to_all(split_up(array, dim, size), axis, 0, 0, tiled=True)
    return jnp.sum(blocks, axis=0)


def total_of(array, axes):
    lines = array.reshape(-1, array.shape[-1])
    padded = padded_to(lines, lax.axis_size(axes))
    whole = gather_directly(sum_at_owner(padded, axes, 0), axes, 0)
    return lax.slice_in_dim(whole, 0, len(lines)).reshape(array.shape)


def tables(cell_index, fraction, extent):
    places = lax.broadcasted_iota(jnp.int32, (cell_index.shape[0], extent), 1)
    lower = jnp.where(places == cell_index[:, None], (1.0 - fraction)[:, None], 0.0)
    return lower + jnp.where(places == cell_index[:, None] + 1, fraction[:, None], 0.0)


def local(row_index, col_index, bin_index, charge, momentum, history, kernel_cols, kernel_rows):
    band_rows = history.shape[1]
    charge_f = charge.astype(jnp.float32)
    cycle_now = history
    kick_sum = jnp.zeros((charge.shape[0], 2), jnp.float32)
    contract_first = (((0,), (0,)), ((), ()))
    for turn_index in range(STEPS):
        bin_now = bin_index[turn_index]
        frac_row = ((bin_now // BINS).astype(jnp.float32) + 0.5) / BINS
        frac_col = ((bin_now % BINS).astype(jnp.float32) + 0.5) / BINS
        row_plain = tables(row_index[turn_index], frac_row, NG)
        row_charged = (row_plain * charge_f[:, None]).astype(jnp.bfloat16)
        row_table = row_plain.astype(jnp.bfloat16)
        col_plain = tables(col_index[turn_index], frac_col, NG)
        col_table = col_plain.astype(jnp.bfloat16)
        partial_grid = lax.dot_general(
            row_charged, col_table, contract_first, preferred_element_type=jnp.float32
        )
        whole_grid = lax.psum(partial_grid, ("hist", "rows", "dom"))
        grid_rows = lax.dynamic_slice_in_dim(
            whole_grid, lax.axis_index("rows") * band_rows, band_rows, 0
        )
        newest = grid_rows.astype(jnp.bfloat16)
        incoming = from_behind(cycle_now[-1], "hist", 1)
        leading = jnp.where(lax.axis_index("hist") == 0, newest, incoming)
        cycle_now = jnp.concatenate([leading[None], cycle_now[:-1]], axis=0)
        mixed_rows = jnp.einsum(
            "kab,kjb->kaj", cycle_now, kernel_cols, preferred_element_type=jnp.float32
        ).astype(jnp.bfloat16)
        partial_field = jnp.einsum(
            "kaci,kaj->icj", kernel_rows, mixed_rows, preferred_element_type=jnp.float32
        )
        summed = total_of(partial_field, ("hist", "rows")).astype(jnp.bfloat16)
        field_full = gather_directly(summed, "dom", 2)
        along_rows = jnp.dot(
            row_table, field_full.reshape(NG, 2 * NG), preferred_element_type=jnp.float32
        )
        kick_now = jnp.sum(along_rows.reshape(-1, 2, NG) * col_plain[:, None, :], axis=2)
        kick_sum = kick_sum + kick_now
    momentum_out = momentum + kick_scale * kick_sum.T
    return (momentum_out, cycle_now)


def solution(mesh):
    in_specs = (
        P(None, ("hist", "rows", "dom")),
        P(None, ("hist", "rows", "dom")),
        P(None, ("hist", "rows", "dom")),
        P(("hist", "rows", "dom")),
        P(None, ("hist", "rows", "dom")),
        P("hist", "rows", None),
        P("hist", "dom", None),
        P("hist", "rows", None, None),
    )
    out_specs = (P(None, ("hist", "rows", "dom")), P("hist", "rows", None))
    return jax.shard_map(local, mesh=mesh, in_specs=in_specs, out_specs=out_specs, check_vma=False)
```

profile of v0, /device:TPU:1, one launch (start us, length us, event | category | flops | bytes accessed | tf_op | source)
XLA Modules:
  0.0 436.7 jit_solution(9039719497938549986)
XLA Ops:
  0.6 1.0 slice_bitcast_fusion
  1.7 4.4 %collective-permute-start = (bf16[64,512]{1,0:T(8,128)(2,1)S(1)}, bf16[64,512]{1,0:T(8,128)(2,1)S(1)}, u32[]{:S(2)}, u32[]{:S(2)}) collective-permute-start(bf16[64,512]{1,0:T(8,128)(2,1)S(1)} %get-tuple-element.24), channel_id=1, source_target_pairs={{0,32},{32,64},{64,96},{96,128},{128,160},{160,192},{192,224},{1,3... | collective-permute-start | bytes 196616 | tf_op jit(solution)/shard_map/ppermute | solution.py:17
  6.1 3.5 collective-permute-start.1
  13.1 2.0 fusion.8
  15.3 3.0 fusion.9
  18.4 3.0 fusion.10
  22.1 3.0 fusion.11
  25.2 131.0 %all-reduce.2 = (bf16[512,512]{1,0:T(8,128)(2,1)}, bf16[512,512]{1,0:T(8,128)(2,1)}, bf16[512,512]{1,0:T(8,128)(2,1)}, bf16[512,512]{1,0:T(8,128)(2,1)}) all-reduce(f32[512,512]{1,0:T(8,128)} %fusion.10, f32[512,512]{1,0:T(8,128)} %fusion.9, ...), channel_id=1, replica_groups=mesh['hist'=8,'rows'=8,'dom'=4] {'hist','rows','dom'}, use_global_device_ids=true, to_apply=%region_6.7 | all-reduce | flops 1048576 | bytes 6291456 | tf_op jit(solution)/shard_map/psum | solution.py:84
  156.1 1.0 slice.73
  159.7 1.0 copy.56
  160.7 10.2 %all-to-all-start.3 = ((f32[64,16,128]{2,1,0:T(8,128)}), f32[64,16,128]{2,1,0:T(8,128)S(1)}, u32[]{:S(2)}, u32[]{:S(2)}) async-start(f32[64,16,128]{2,1,0:T(8,128)} %bitcast.124), calls=%async_computation.3 | async-start | bytes 1048576 | tf_op jit(solution)/shard_map/all_to_all | solution.py:49
  170.9 2.9 collective-permute-start.2
  173.8 6.2 %collective-permute-done.2 = bf16[64,512]{1,0:T(8,128)(2,1)S(1)} collective-permute-done((bf16[64,512]{1,0:T(8,128)(2,1)S(1)}, bf16[64,512]{1,0:T(8,128)(2,1)S(1)}, u32[]{:S(2)}, u32[]{:S(2)}) %collective-permute-start.2) | collective-permute-done | bytes 65568 | tf_op jit(solution)/shard_map/ppermute | solution.py:17
  180.9 1.6 convolution_bitcast_fusion.1
  182.5 2.1 copy.61
  184.5 1.8 all-to-all-done.3
  186.3 14.7 %all-to-all-start.6 = ((f32[64,16,128]{2,1,0:T(8,128)}), f32[64,16,128]{2,1,0:T(8,128)}, u32[]{:S(2)}, u32[]{:S(2)}) async-start(f32[64,16,128]{2,1,0:T(8,128)} %bitcast.123), calls=%async_computation.6 | async-start | bytes 1048576 | tf_op jit(solution)/shard_map/all_to_all | solution.py:49
  201.1 2.8 collective-permute-start.3
  203.9 5.4 %collective-permute-done.3 = bf16[64,512]{1,0:T(8,128)(2,1)S(1)} collective-permute-done((bf16[64,512]{1,0:T(8,128)(2,1)S(1)}, bf16[64,512]{1,0:T(8,128)(2,1)S(1)}, u32[]{:S(2)}, u32[]{:S(2)}) %collective-permute-start.3) | collective-permute-done | bytes 65568 | tf_op jit(solution)/shard_map/ppermute | solution.py:17
  210.2 0.9 fusion.72
  211.1 2.6 convolution_bitcast_fusion
  213.7 2.0 copy.66
  215.8 16.9 %all-to-all-start.9 = ((f32[64,16,128]{2,1,0:T(8,128)}), f32[64,16,128]{2,1,0:T(8,128)}, u32[]{:S(2)}, u32[]{:S(2)}) async-start(f32[64,16,128]{2,1,0:T(8,128)} %bitcast.125), calls=%async_computation.9 | async-start | bytes 1048576 | tf_op jit(solution)/shard_map/all_to_all | solution.py:49
  232.7 1.5 convolution_bitcast_fusion.3
  234.2 2.0 copy.51
  236.3 11.1 %all-to-all-done.9 = f32[64,16,128]{2,1,0:T(8,128)} async-done(((f32[64,16,128]{2,1,0:T(8,128)}), f32[64,16,128]{2,1,0:T(8,128)}, u32[]{:S(2)}, u32[]{:S(2)}) %all-to-all-start.9) | async-done | bytes 524320 | tf_op jit(solution)/shard_map/all_to_all | solution.py:49
  247.4 9.0 %all-to-all-start = ((f32[64,16,128]{2,1,0:T(8,128)}), f32[64,16,128]{2,1,0:T(8,128)S(1)}, u32[]{:S(2)}, u32[]{:S(2)}) async-start(f32[64,16,128]{2,1,0:T(8,128)} %bitcast.10), calls=%async_computation | async-start | bytes 1048576 | tf_op jit(solution)/shard_map/all_to_all | solution.py:49
  256.5 14.4 %all-to-all-done = f32[64,16,128]{2,1,0:T(8,128)S(1)} async-done(((f32[64,16,128]{2,1,0:T(8,128)}), f32[64,16,128]{2,1,0:T(8,128)S(1)}, u32[]{:S(2)}, u32[]{:S(2)}) %all-to-all-start) | async-done | bytes 524320 | tf_op jit(solution)/shard_map/all_to_all | solution.py:49
  271.6 9.4 %all-to-all-start.4 = ((bf16[64,16,128]{2,1,0:T(8,128)(2,1)}), bf16[64,16,128]{2,1,0:T(8,128)(2,1)S(1)}, u32[]{:S(2)}, u32[]{:S(2)}) async-start(bf16[64,16,128]{2,1,0:T(8,128)(2,1)} %broadcast_in_dim.175), calls=%async_computation.4 | async-start | bytes 524288 | tf_op jit(solution)/shard_map/all_to_all | solution.py:35
  281.0 1.1 reduce_sum.76
  282.1 10.8 %all-to-all-done.4 = bf16[64,16,128]{2,1,0:T(8,128)(2,1)S(1)} async-done(((bf16[64,16,128]{2,1,0:T(8,128)(2,1)}), bf16[64,16,128]{2,1,0:T(8,128)(2,1)S(1)}, u32[]{:S(2)}, u32[]{:S(2)}) %all-to-all-start.4) | async-done | bytes 262176 | tf_op jit(solution)/shard_map/all_to_all | solution.py:35
  293.6 5.1 %all-to-all-start.7 = ((bf16[64,16,128]{2,1,0:T(8,128)(2,1)}), bf16[64,16,128]{2,1,0:T(8,128)(2,1)S(1)}, u32[]{:S(2)}, u32[]{:S(2)}) async-start(bf16[64,16,128]{2,1,0:T(8,128)(2,1)} %broadcast_in_dim.182), calls=%async_computation.7 | async-start | bytes 524288 | tf_op jit(solution)/shard_map/all_to_all | solution.py:35
  298.7 1.1 reduce_sum.78
  299.9 10.7 %all-to-all-done.7 = bf16[64,16,128]{2,1,0:T(8,128)(2,1)S(1)} async-done(((bf16[64,16,128]{2,1,0:T(8,128)(2,1)}), bf16[64,16,128]{2,1,0:T(8,128)(2,1)S(1)}, u32[]{:S(2)}, u32[]{:S(2)}) %all-to-all-start.7) | async-done | bytes 262176 | tf_op jit(solution)/shard_map/all_to_all | solution.py:35
  311.3 5.1 %all-to-all-start.10 = ((bf16[64,16,128]{2,1,0:T(8,128)(2,1)}), bf16[64,16,128]{2,1,0:T(8,128)(2,1)S(1)}, u32[]{:S(2)}, u32[]{:S(2)}) async-start(bf16[64,16,128]{2,1,0:T(8,128)(2,1)} %broadcast_in_dim.189), calls=%async_computation.10 | async-start | bytes 524288 | tf_op jit(solution)/shard_map/all_to_all | solution.py:35
  316.5 11.8 %all-to-all-done.10 = bf16[64,16,128]{2,1,0:T(8,128)(2,1)S(1)} async-done(((bf16[64,16,128]{2,1,0:T(8,128)(2,1)}), bf16[64,16,128]{2,1,0:T(8,128)(2,1)S(1)}, u32[]{:S(2)}, u32[]{:S(2)}) %all-to-all-start.10) | async-done | bytes 262176 | tf_op jit(solution)/shard_map/all_to_all | solution.py:35
  329.1 5.1 %all-to-all-start.1 = ((bf16[64,16,128]{2,1,0:T(8,128)(2,1)}), bf16[64,16,128]{2,1,0:T(8,128)(2,1)S(1)}, u32[]{:S(2)}, u32[]{:S(2)}) async-start(bf16[64,16,128]{2,1,0:T(8,128)(2,1)} %broadcast_in_dim.168), calls=%async_computation.1 | async-start | bytes 524288 | tf_op jit(solution)/shard_map/all_to_all | solution.py:35
  334.3 11.8 %all-to-all-done.1 = bf16[64,16,128]{2,1,0:T(8,128)(2,1)S(1)} async-done(((bf16[64,16,128]{2,1,0:T(8,128)(2,1)}), bf16[64,16,128]{2,1,0:T(8,128)(2,1)S(1)}, u32[]{:S(2)}, u32[]{:S(2)}) %all-to-all-start.1) | async-done | bytes 262176 | tf_op jit(solution)/shard_map/all_to_all | solution.py:35
  346.1 1.1 broadcast_in_dim.176
  347.2 10.2 %all-to-all-start.5 = ((bf16[4,512,2,128]{1,3,2,0:T(8,128)(2,1)}), bf16[4,512,2,128]{1,3,2,0:T(8,128)(2,1)S(1)}, u32[]{:S(2)}, u32[]{:S(2)}) async-start(bf16[4,512,2,128]{1,3,2,0:T(8,128)(2,1)} %broadcast_in_dim.176), calls=%async_computation.5 | async-start | bytes 2097152 | tf_op jit(solution)/shard_map/all_to_all | solution.py:35
  357.6 13.4 %all-to-all-done.5 = bf16[4,512,2,128]{1,3,2,0:T(8,128)(2,1)S(1)} async-done(((bf16[4,512,2,128]{1,3,2,0:T(8,128)(2,1)}), bf16[4,512,2,128]{1,3,2,0:T(8,128)(2,1)S(1)}, u32[]{:S(2)}, u32[]{:S(2)}) %all-to-all-start.5) | async-done | bytes 1048608 | tf_op jit(solution)/shard_map/all_to_all | solution.py:35
  371.0 1.2 broadcast_in_dim.183
  372.3 5.1 %all-to-all-start.8 = ((bf16[4,512,2,128]{1,3,2,0:T(8,128)(2,1)}), bf16[4,512,2,128]{1,3,2,0:T(8,128)(2,1)}, u32[]{:S(2)}, u32[]{:S(2)}) async-start(bf16[4,512,2,128]{1,3,2,0:T(8,128)(2,1)} %broadcast_in_dim.183), calls=%async_computation.8 | async-start | bytes 2097152 | tf_op jit(solution)/shard_map/all_to_all | solution.py:35
  378.1 1.8 select_add_fusion.2
  379.9 1.1 copy.67
  381.0 10.1 %all-to-all-done.8 = bf16[4,512,2,128]{1,3,2,0:T(8,128)(2,1)} async-done(((bf16[4,512,2,128]{1,3,2,0:T(8,128)(2,1)}), bf16[4,512,2,128]{1,3,2,0:T(8,128)(2,1)}, u32[]{:S(2)}, u32[]{:S(2)}) %all-to-all-start.8) | async-done | bytes 1048608 | tf_op jit(solution)/shard_map/all_to_all | solution.py:35
  391.1 1.1 broadcast_in_dim.190
  392.2 5.1 %all-to-all-start.11 = ((bf16[4,512,2,128]{1,3,2,0:T(8,128)(2,1)}), bf16[4,512,2,128]{1,3,2,0:T(8,128)(2,1)}, u32[]{:S(2)}, u32[]{:S(2)}) async-start(bf16[4,512,2,128]{1,3,2,0:T(8,128)(2,1)} %broadcast_in_dim.190), calls=%async_computation.11 | async-start | bytes 2097152 | tf_op jit(solution)/shard_map/all_to_all | solution.py:35
  397.3 1.8 select_add_fusion
  399.1 1.9 copy.59
  401.0 3.1 copy.64
  404.1 1.9 copy.69
  406.6 1.8 copy.54
  408.7 1.4 copy.58
  410.1 1.3 copy.63
  411.5 2.3 multiply_reduce_fusion.2
  413.8 1.1 broadcast_in_dim.169
  414.9 3.8 all-to-all-start.2
  418.7 1.4 copy.68
  420.6 2.3 multiply_reduce_fusion.1
  423.0 2.3 multiply_reduce_fusion
  425.3 7.0 %all-to-all-done.2 = bf16[4,512,2,128]{1,3,2,0:T(8,128)(2,1)S(1)} async-done(((bf16[4,512,2,128]{1,3,2,0:T(8,128)(2,1)}), bf16[4,512,2,128]{1,3,2,0:T(8,128)(2,1)S(1)}, u32[]{:S(2)}, u32[]{:S(2)}) %all-to-all-start.2) | async-done | bytes 1048608 | tf_op jit(solution)/shard_map/all_to_all | solution.py:35
  432.4 1.5 copy-done.4
  433.9 2.2 multiply_reduce_fusion.3
  (169 shorter events, 14.7 us)
Async XLA Ops:
  0.6 158.3 %copy-start = (bf16[8,64,2,512]{3,2,1,0:T(2,128)(2,1)S(1)}, bf16[8,64,2,512]{3,2,1,0:T(2,128)(2,1)}, u32[]{:S(2)}) copy-start(bf16[8,64,2,512]{3,2,1,0:T(2,128)(2,1)} %param.15) | copy-start | bytes 3145732
  1.7 155.5 %collective-permute-start = (bf16[64,512]{1,0:T(8,128)(2,1)S(1)}, bf16[64,512]{1,0:T(8,128)(2,1)S(1)}, u32[]{:S(2)}, u32[]{:S(2)}) collective-permute-start(bf16[64,512]{1,0:T(8,128)(2,1)S(1)} %get-tuple-element.24), channel_id=1, source_target_pairs={{0,32},{32,64},{64,96},{96,128},{128,160},{160,192},{192,224},{1,3... | collective-permute-start | bytes 196616 | tf_op jit(solution)/shard_map/ppermute | solution.py:17
  6.1 152.0 %collective-permute-start.1 = (bf16[64,512]{1,0:T(8,128)(2,1)S(1)}, bf16[64,512]{1,0:T(8,128)(2,1)S(1)}, u32[]{:S(2)}, u32[]{:S(2)}) collective-permute-start(bf16[64,512]{1,0:T(8,128)(2,1)S(1)} %get-tuple-element.23), channel_id=1, source_target_pairs={{0,32},{32,64},{64,96},{96,128},{128,160},{160,192},{192,224},{1,3... | collective-permute-start | bytes 196616 | tf_op jit(solution)/shard_map/ppermute | solution.py:17
  10.5 4.6 %copy-start.35 = (s32[1,1024]{1,0:T(1,128)}, s32[1,1024]{1,0:T(1,128)S(1)}, u32[]{:S(2)}) copy-start(s32[1,1024]{1,0:T(1,128)S(1)} %get-tuple-element.32) | copy-start | bytes 12292
  10.5 4.7 %copy-start.41 = (s32[1,1024]{1,0:T(1,128)}, s32[1,1024]{1,0:T(1,128)S(1)}, u32[]{:S(2)}) copy-start(s32[1,1024]{1,0:T(1,128)S(1)} %get-tuple-element.31) | copy-start | bytes 12292
  10.5 7.9 %copy-start.39 = (s32[1,1024]{1,0:T(1,128)}, s32[1,1024]{1,0:T(1,128)S(1)}, u32[]{:S(2)}) copy-start(s32[1,1024]{1,0:T(1,128)S(1)} %get-tuple-element.33) | copy-start | bytes 12292
  10.5 11.0 %copy-start.37 = (s32[1,1024]{1,0:T(1,128)}, s32[1,1024]{1,0:T(1,128)S(1)}, u32[]{:S(2)}) copy-start(s32[1,1024]{1,0:T(1,128)S(1)} %get-tuple-element.30) | copy-start | bytes 12292
  12.3 2.8 copy-start.11
  12.4 2.8 copy-start.13
  12.4 2.8 copy-start.44
  12.4 2.8 copy-start.46
  15.2 3.1 copy-start.15
  15.2 3.1 copy-start.17
  15.2 3.1 copy-start.56
  15.2 3.1 copy-start.58
  15.2 3.1 copy-start.29
  15.3 3.1 copy-start.66
  18.4 3.1 copy-start.23
  18.4 3.1 copy-start.25
  18.4 3.1 copy-start.48
  18.4 3.1 copy-start.50
  18.4 3.0 copy-start.33
  18.4 3.0 copy-start.62
  25.2 133.8 %copy-start.2 = (bf16[8,128,512]{2,1,0:T(8,128)(2,1)S(1)}, bf16[8,128,512]{2,1,0:T(8,128)(2,1)}, u32[]{:S(2)}) copy-start(bf16[8,128,512]{2,1,0:T(8,128)(2,1)} %param.14) | copy-start | bytes 3145732
  160.7 25.6 %all-to-all-start.3 = ((f32[64,16,128]{2,1,0:T(8,128)}), f32[64,16,128]{2,1,0:T(8,128)S(1)}, u32[]{:S(2)}, u32[]{:S(2)}) async-start(f32[64,16,128]{2,1,0:T(8,128)} %bitcast.124), calls=%async_computation.3 | async-start | bytes 1048576 | tf_op jit(solution)/shard_map/all_to_all | solution.py:49
  170.9 9.1 %collective-permute-start.2 = (bf16[64,512]{1,0:T(8,128)(2,1)S(1)}, bf16[64,512]{1,0:T(8,128)(2,1)S(1)}, u32[]{:S(2)}, u32[]{:S(2)}) collective-permute-start(bf16[64,512]{1,0:T(8,128)(2,1)S(1)} %get-tuple-element.25), channel_id=1, source_target_pairs={{0,32},{32,64},{64,96},{96,128},{128,160},{160,192},{192,224},{1,3... | collective-permute-start | bytes 196616 | tf_op jit(solution)/shard_map/ppermute | solution.py:17
  186.3 29.4 %all-to-all-start.6 = ((f32[64,16,128]{2,1,0:T(8,128)}), f32[64,16,128]{2,1,0:T(8,128)}, u32[]{:S(2)}, u32[]{:S(2)}) async-start(f32[64,16,128]{2,1,0:T(8,128)} %bitcast.123), calls=%async_computation.6 | async-start | bytes 1048576 | tf_op jit(solution)/shard_map/all_to_all | solution.py:49
  201.1 8.3 %collective-permute-start.3 = (bf16[64,512]{1,0:T(8,128)(2,1)S(1)}, bf16[64,512]{1,0:T(8,128)(2,1)S(1)}, u32[]{:S(2)}, u32[]{:S(2)}) collective-permute-start(bf16[64,512]{1,0:T(8,128)(2,1)S(1)} %get-tuple-element.22), channel_id=1, source_target_pairs={{0,32},{32,64},{64,96},{96,128},{128,160},{160,192},{192,224},{1,3... | collective-permute-start | bytes 196616 | tf_op jit(solution)/shard_map/ppermute | solution.py:17
  215.8 31.6 %all-to-all-start.9 = ((f32[64,16,128]{2,1,0:T(8,128)}), f32[64,16,128]{2,1,0:T(8,128)}, u32[]{:S(2)}, u32[]{:S(2)}) async-start(f32[64,16,128]{2,1,0:T(8,128)} %bitcast.125), calls=%async_computation.9 | async-start | bytes 1048576 | tf_op jit(solution)/shard_map/all_to_all | solution.py:49
  247.4 23.5 %all-to-all-start = ((f32[64,16,128]{2,1,0:T(8,128)}), f32[64,16,128]{2,1,0:T(8,128)S(1)}, u32[]{:S(2)}, u32[]{:S(2)}) async-start(f32[64,16,128]{2,1,0:T(8,128)} %bitcast.10), calls=%async_computation | async-start | bytes 1048576 | tf_op jit(solution)/shard_map/all_to_all | solution.py:49
  271.6 21.3 %all-to-all-start.4 = ((bf16[64,16,128]{2,1,0:T(8,128)(2,1)}), bf16[64,16,128]{2,1,0:T(8,128)(2,1)S(1)}, u32[]{:S(2)}, u32[]{:S(2)}) async-start(bf16[64,16,128]{2,1,0:T(8,128)(2,1)} %broadcast_in_dim.175), calls=%async_computation.4 | async-start | bytes 524288 | tf_op jit(solution)/shard_map/all_to_all | solution.py:35
  293.6 17.0 %all-to-all-start.7 = ((bf16[64,16,128]{2,1,0:T(8,128)(2,1)}), bf16[64,16,128]{2,1,0:T(8,128)(2,1)S(1)}, u32[]{:S(2)}, u32[]{:S(2)}) async-start(bf16[64,16,128]{2,1,0:T(8,128)(2,1)} %broadcast_in_dim.182), calls=%async_computation.7 | async-start | bytes 524288 | tf_op jit(solution)/shard_map/all_to_all | solution.py:35
  311.3 16.9 %all-to-all-start.10 = ((bf16[64,16,128]{2,1,0:T(8,128)(2,1)}), bf16[64,16,128]{2,1,0:T(8,128)(2,1)S(1)}, u32[]{:S(2)}, u32[]{:S(2)}) async-start(bf16[64,16,128]{2,1,0:T(8,128)(2,1)} %broadcast_in_dim.189), calls=%async_computation.10 | async-start | bytes 524288 | tf_op jit(solution)/shard_map/all_to_all | solution.py:35
  328.2 19.0 %copy-start.10 = (bf16[64,16,128]{2,1,0:T(8,128)(2,1)}, bf16[64,16,128]{2,1,0:T(8,128)(2,1)S(1)}, u32[]{:S(2)}) copy-start(bf16[64,16,128]{2,1,0:T(8,128)(2,1)S(1)} %all-to-all-done.10) | copy-start | bytes 786436
  329.1 17.0 %all-to-all-start.1 = ((bf16[64,16,128]{2,1,0:T(8,128)(2,1)}), bf16[64,16,128]{2,1,0:T(8,128)(2,1)S(1)}, u32[]{:S(2)}, u32[]{:S(2)}) async-start(bf16[64,16,128]{2,1,0:T(8,128)(2,1)} %broadcast_in_dim.168), calls=%async_computation.1 | async-start | bytes 524288 | tf_op jit(solution)/shard_map/all_to_all | solution.py:35
  347.2 23.8 %all-to-all-start.5 = ((bf16[4,512,2,128]{1,3,2,0:T(8,128)(2,1)}), bf16[4,512,2,128]{1,3,2,0:T(8,128)(2,1)S(1)}, u32[]{:S(2)}, u32[]{:S(2)}) async-start(bf16[4,512,2,128]{1,3,2,0:T(8,128)(2,1)} %broadcast_in_dim.176), calls=%async_computation.5 | async-start | bytes 2097152 | tf_op jit(solution)/shard_map/all_to_all | solution.py:35
  357.4 20.0 %copy-start.16 = (f32[1024]{0:T(1024)S(1)}, f32[1024]{0:T(1024)}, u32[]{:S(2)}) copy-start(f32[1024]{0:T(1024)} %copy-done.15) | copy-start | bytes 12292
  357.4 20.0 %copy-start.18 = (f32[1024]{0:T(1024)S(1)}, f32[1024]{0:T(1024)}, u32[]{:S(2)}) copy-start(f32[1024]{0:T(1024)} %copy-done.17) | copy-start | bytes 12292
  357.4 20.0 %copy-start.30 = (s32[1024]{0:T(1024)S(1)}, s32[1024]{0:T(1024)}, u32[]{:S(2)}) copy-start(s32[1024]{0:T(1024)} %copy-done.29) | copy-start | bytes 12292
  372.2 5.9 %copy-start.24 = (f32[1024]{0:T(1024)S(1)}, f32[1024]{0:T(1024)}, u32[]{:S(2)}) copy-start(f32[1024]{0:T(1024)} %copy-done.23) | copy-start | bytes 12292
  372.2 5.9 %copy-start.26 = (f32[1024]{0:T(1024)S(1)}, f32[1024]{0:T(1024)}, u32[]{:S(2)}) copy-start(f32[1024]{0:T(1024)} %copy-done.25) | copy-start | bytes 12292
  372.2 5.9 %copy-start.34 = (s32[1024]{0:T(1024)S(1)}, s32[1024]{0:T(1024)}, u32[]{:S(2)}) copy-start(s32[1024]{0:T(1024)} %copy-done.33) | copy-start | bytes 12292
  372.3 18.8 %all-to-all-start.8 = ((bf16[4,512,2,128]{1,3,2,0:T(8,128)(2,1)}), bf16[4,512,2,128]{1,3,2,0:T(8,128)(2,1)}, u32[]{:S(2)}, u32[]{:S(2)}) async-start(bf16[4,512,2,128]{1,3,2,0:T(8,128)(2,1)} %broadcast_in_dim.183), calls=%async_computation.8 | async-start | bytes 2097152 | tf_op jit(solution)/shard_map/all_to_all | solution.py:35
  379.9 17.4 %copy-start.20 = (f32[1024]{0:T(1024)S(1)}, f32[1024]{0:T(1024)}, u32[]{:S(2)}) copy-start(f32[1024]{0:T(1024)} %copy-done.19) | copy-start | bytes 12292
  379.9 17.4 %copy-start.22 = (f32[1024]{0:T(1024)S(1)}, f32[1024]{0:T(1024)}, u32[]{:S(2)}) copy-start(f32[1024]{0:T(1024)} %copy-done.21) | copy-start | bytes 12292
  379.9 17.4 %copy-start.32 = (s32[1024]{0:T(1024)S(1)}, s32[1024]{0:T(1024)}, u32[]{:S(2)}) copy-start(s32[1024]{0:T(1024)} %copy-done.31) | copy-start | bytes 12292
  392.2 21.5 %all-to-all-start.11 = ((bf16[4,512,2,128]{1,3,2,0:T(8,128)(2,1)}), bf16[4,512,2,128]{1,3,2,0:T(8,128)(2,1)}, u32[]{:S(2)}, u32[]{:S(2)}) async-start(bf16[4,512,2,128]{1,3,2,0:T(8,128)(2,1)} %broadcast_in_dim.190), calls=%async_computation.11 | async-start | bytes 2097152 | tf_op jit(solution)/shard_map/all_to_all | solution.py:35
  401.0 3.1 copy-start.1
  408.6 2.8 copy-start.7
  408.6 2.8 copy-start.42
  408.6 2.8 copy-start.57
  408.6 2.8 copy-start.59
  408.6 2.8 copy-start.67
  414.9 5.2 %copy-start.40 = (s32[1,1024]{1,0:T(1,128)S(1)}, s32[1,1024]{1,0:T(1,128)}, u32[]{:S(2)}) copy-start(s32[1,1024]{1,0:T(1,128)} %copy-done.39) | copy-start | bytes 12292
  414.9 5.3 %copy-start.49 = (f32[1024]{0:T(1024)S(1)}, f32[1024]{0:T(1024)}, u32[]{:S(2)}) copy-start(f32[1024]{0:T(1024)} %copy-done.48) | copy-start | bytes 12292
  414.9 5.3 %copy-start.51 = (f32[1024]{0:T(1024)S(1)}, f32[1024]{0:T(1024)}, u32[]{:S(2)}) copy-start(f32[1024]{0:T(1024)} %copy-done.50) | copy-start | bytes 12292
  414.9 5.3 %copy-start.63 = (s32[1024]{0:T(1024)S(1)}, s32[1024]{0:T(1024)}, u32[]{:S(2)}) copy-start(s32[1024]{0:T(1024)} %copy-done.62) | copy-start | bytes 12292
  414.9 17.4 %all-to-all-start.2 = ((bf16[4,512,2,128]{1,3,2,0:T(8,128)(2,1)}), bf16[4,512,2,128]{1,3,2,0:T(8,128)(2,1)S(1)}, u32[]{:S(2)}, u32[]{:S(2)}) async-start(bf16[4,512,2,128]{1,3,2,0:T(8,128)(2,1)} %broadcast_in_dim.169), calls=%async_computation.2 | async-start | bytes 2097152 | tf_op jit(solution)/shard_map/all_to_all | solution.py:35
  420.6 2.3 copy-start.55
  420.6 2.3 copy-start.65
  422.9 9.4 %copy-start.36 = (s32[1,1024]{1,0:T(1,128)S(1)}, s32[1,1024]{1,0:T(1,128)}, u32[]{:S(2)}) copy-start(s32[1,1024]{1,0:T(1,128)} %copy-done.35) | copy-start | bytes 12292
  423.0 9.4 %copy-start.45 = (f32[1024]{0:T(1024)S(1)}, f32[1024]{0:T(1024)}, u32[]{:S(2)}) copy-start(f32[1024]{0:T(1024)} %copy-done.44) | copy-start | bytes 12292
  423.0 9.4 %copy-start.47 = (f32[1024]{0:T(1024)S(1)}, f32[1024]{0:T(1024)}, u32[]{:S(2)}) copy-start(f32[1024]{0:T(1024)} %copy-done.46) | copy-start | bytes 12292
  423.0 9.4 %copy-start.61 = (s32[1024]{0:T(1024)S(1)}, s32[1024]{0:T(1024)}, u32[]{:S(2)}) copy-start(s32[1024]{0:T(1024)} %copy-done.60) | copy-start | bytes 12292
  (20 other events, 30.3 us)
where the time goes:
time: 439 us; the launch traced here: 437 us
  blocking collectives  131 us (30%)
  waiting for transfers between devices  115 us (26%)
  starting transfers between devices  113 us (26%)
  local copies, waits for them, and re-layouts  36.9 us (8%)
  matrix products  26.5 us (6%)
  other arithmetic  12.9 us (3%)
    psum x1, blocking collectives, local(): whole_grid = lax.psum(partial_grid, ('hist', 'rows', 'dom'))  131 us
    all_to_all x8, waiting for transfers between devices, from_everyone(): return lax.all_to_all(copies, axis, split_axis=0, concat_axis=0, tiled=True)  75.6 us
    all_to_all x4, starting transfers between devices, sum_at_owner(): blocks = lax.all_to_all(split_up(array, dim, size), axis, 0, 0, tiled=True)  50.8 us
    all_to_all x8, starting transfers between devices, from_everyone(): return lax.all_to_all(copies, axis, split_axis=0, concat_axis=0, tiled=True)  48.7 us
    all_to_all x4, waiting for transfers between devices, sum_at_owner(): blocks = lax.all_to_all(split_up(array, dim, size), axis, 0, 0, tiled=True)  27.3 us
    ppermute x4, starting transfers between devices, from_behind(): return lax.ppermute(array, axis, pairs)  13.7 us
    ppermute x4, waiting for transfers between devices, from_behind(): return lax.ppermute(array, axis, pairs)  11.6 us
    dot_general x4, matrix products, local(): lax.dot_general(row_charged, col_table, contract_first, preferred_element...  11.1 us
  transfers between devices with their start and end apart: 16, of which 13 were waited for; matrix products, arithmetic and copies ran while one was open for 14% of the time, Pallas kernels for 0%

commit v1 on v0

v1 whole, which is shorter than its diff:
```python
import jax
import jax.numpy as jnp
from jax import lax
from jax.experimental import pallas as pl
from jax.experimental.pallas import tpu as pltpu
from jax.sharding import PartitionSpec as P

NG = 512
BINS = 16
STEPS = 4
LANES = 128

kick_scale = 0.5
f32 = jnp.float32
bf16 = jnp.bfloat16


def swap(array, axes):
    return lax.all_to_all(array, axes, split_axis=0, concat_axis=0, tiled=True)


def to_all(array, axes):
    copies = jnp.broadcast_to(array, (lax.axis_size(axes), *array.shape))
    return swap(copies, axes)


def hat(places, at):
    return jnp.maximum(1.0 - jnp.abs(places - at), 0.0)


def unpack(particles, source):
    lines = particles.shape[1] // 4

    def field(which):
        rows = [particles[source, which * lines + k : which * lines + k + 1, :] for k in range(lines)]
        return jnp.concatenate(rows, axis=1)

    bins = field(2)
    row_bin = jnp.floor(bins * (1.0 / BINS))
    col_bin = bins - row_bin * BINS
    at_row = field(0) + (row_bin + 0.5) * (1.0 / BINS)
    at_col = field(1) + (col_bin + 0.5) * (1.0 / BINS)
    return at_row, at_col, field(3)


def deposit_kernel(particles, out, total):
    source = pl.program_id(0)
    at_row, at_col, charge = unpack(particles, 0)
    places = lax.broadcasted_iota(jnp.int32, (NG, at_row.shape[1]), 0).astype(f32)
    row_table = (hat(places, at_row) * charge).astype(bf16)
    col_table = hat(places, at_col).astype(bf16)
    part = lax.dot_general(row_table, col_table, (((1,), (1,)), ((), ())), preferred_element_type=f32)

    @pl.when(source == 0)
    def _():
        total[...] = part

    @pl.when(source > 0)
    def _():
        total[...] += part

    @pl.when(source == pl.num_programs(0) - 1)
    def _():
        out[...] = total[...].reshape(out.shape).astype(bf16)


def deposit(particles, bands):
    sources, lines, _ = particles.shape
    return pl.pallas_call(
        deposit_kernel,
        grid=(sources,),
        in_specs=[pl.BlockSpec((1, lines, LANES), lambda i: (i, 0, 0))],
        out_specs=pl.BlockSpec((bands, NG // bands, NG), lambda i: (0, 0, 0)),
        out_shape=jax.ShapeDtypeStruct((bands, NG // bands, NG), bf16),
        scratch_shapes=[pltpu.VMEM((NG, NG), f32)],
        compiler_params=pltpu.CompilerParams(vmem_limit_bytes=48 << 20),
        name="deposit",
    )(particles)


def kick_kernel(particles, field, out):
    at_row, at_col, _ = unpack(particles, 0)
    shape = (NG, at_row.shape[1])
    places = lax.broadcasted_iota(jnp.int32, shape, 0)
    row_table = hat(places.astype(f32), at_row).astype(bf16)
    column = ((places >> 4) & 3) * 128 + (places >> 6) * 16 + (places & 15)
    col_table = hat(column.astype(f32), at_col)
    lines = shape[1] // LANES
    for comp in range(2):
        along = jnp.dot(field[:, comp * NG : (comp + 1) * NG], row_table, preferred_element_type=f32)
        kick = jnp.sum(along * col_table, axis=0, keepdims=True)
        for k in range(lines):
            out[0, comp * lines + k : comp * lines + k + 1, :] = kick[:, k * LANES : (k + 1) * LANES]


def kicks(particles, field):
    sources, lines, _ = particles.shape
    return pl.pallas_call(
        kick_kernel,
        grid=(sources,),
        in_specs=[
            pl.BlockSpec((1, lines, LANES), lambda i: (i, 0, 0)),
            pl.BlockSpec((NG, 2 * NG), lambda i: (0, 0)),
        ],
        out_specs=pl.BlockSpec((1, lines // 2, LANES), lambda i: (i, 0, 0)),
        out_shape=jax.ShapeDtypeStruct((sources, lines // 2, LANES), f32),
        compiler_params=pltpu.CompilerParams(vmem_limit_bytes=48 << 20),
        name="kicks",
    )(particles, field)


def old_mixed_kernel(history, cols, out):
    lags, band, _ = history.shape
    for lag in range(1, lags):
        steps = min(lag, STEPS)
        grids = history[lag - steps : lag].reshape(steps * band, NG)
        mixed = lax.dot_general(grids, cols[lag], (((1,), (1,)), ((), ())), preferred_element_type=f32)
        mixed = mixed.astype(bf16).reshape(steps, band, mixed.shape[1])
        for step in range(steps):
            out[step, lag] = mixed[steps - 1 - step]
    for step in range(STEPS):
        for lag in range(step + 1):
            out[step, lag] = jnp.zeros(out.shape[2:], bf16)


def old_mixed(history, cols):
    lags, band, _ = history.shape
    return pl.pallas_call(
        old_mixed_kernel,
        out_shape=jax.ShapeDtypeStruct((STEPS, lags, band, cols.shape[1]), bf16),
        compiler_params=pltpu.CompilerParams(vmem_limit_bytes=48 << 20),
        name="old_mixed",
    )(history, cols)


def field_kernel(first, fresh, incoming, cols, rows, mixed_old, out):
    band = incoming.shape[1]
    ahead = [jnp.where(first[0] == 1, fresh[STEPS - 1 - n], incoming[n]) for n in range(STEPS)]
    grids = jnp.concatenate(ahead, axis=0)
    wide = cols.shape[1]
    parts = [[] for _ in range(STEPS)]
    for lag in range(STEPS):
        count = STEPS - lag
        mixed = lax.dot_general(
            grids[lag * band :], cols[lag], (((1,), (1,)), ((), ())), preferred_element_type=f32
        ).astype(bf16)
        for n in range(count):
            parts[STEPS - 1 - n].append(mixed[n * band : (n + 1) * band])
    bands = out.shape[0] // STEPS
    share = wide // bands
    for step in range(STEPS):
        lines = parts[step] + [mixed_old[step, lag] for lag in range(step + 1, mixed_old.shape[1])]
        lhs = jnp.concatenate(lines, axis=0)
        field = lax.dot_general(lhs, rows[...], (((0,), (0,)), ((), ())), preferred_element_type=f32)
        field = field.astype(bf16)
        for band_to in range(bands):
            out[band_to * STEPS + step] = field[band_to * share : (band_to + 1) * share]


def field_parts(first, fresh, incoming, cols, rows, mixed_old, bands):
    wide = cols.shape[1]
    vmem = pl.BlockSpec(memory_space=pltpu.VMEM)
    return pl.pallas_call(
        field_kernel,
        in_specs=[pl.BlockSpec(memory_space=pltpu.SMEM)] + [vmem] * 5,
        out_specs=vmem,
        out_shape=jax.ShapeDtypeStruct((bands * STEPS, wide // bands, rows.shape[1]), bf16),
        compiler_params=pltpu.CompilerParams(vmem_limit_bytes=48 << 20),
        name="field_parts",
    )(first, fresh, incoming, cols, rows, mixed_old)


def local(row_index, col_index, bin_index, charge, momentum, history, kernel_cols, kernel_rows):
    lags, band, _ = history.shape
    count = charge.shape[0]
    bands = NG // band
    lines = count // LANES
    hist_at = lax.axis_index("hist")
    hist_size = lax.axis_size("hist")

    fields = [row_index.astype(f32), col_index.astype(f32), bin_index.astype(f32)]
    fields.append(jnp.broadcast_to(charge.astype(f32), (STEPS, count)))
    packed = jnp.stack([x.reshape(STEPS, lines, LANES) for x in fields], axis=1)
    particles = swap(packed.reshape(STEPS, 4 * lines, LANES), "dom")

    incoming = lax.ppermute(history[lags - STEPS :], "hist", [(i, i + 1) for i in range(hist_size - 1)])
    mixed_old = old_mixed(history, kernel_cols)
    rows_flat = kernel_rows.reshape(lags * band, 2 * NG)

    grid = deposit(particles, bands)
    by_band = jnp.sum(swap(grid, "rows").astype(f32), axis=0).astype(bf16)
    density = jnp.sum(to_all(by_band, "hist").astype(f32), axis=0).astype(bf16)
    fresh = to_all(density, "dom")

    first = (hist_at == 0).astype(jnp.int32).reshape(1)
    partial = field_parts(first, fresh, incoming, kernel_cols[:STEPS], rows_flat, mixed_old, bands)
    received = swap(partial, ("rows", "dom"))
    share = received.shape[1]
    by_column = jnp.sum(received.reshape(bands, STEPS * share, 2 * NG).astype(f32), axis=0).astype(bf16)
    summed = jnp.sum(to_all(by_column, "hist").astype(f32), axis=0).astype(bf16)
    field = to_all(summed, "rows").reshape(NG, 2 * NG)

    kick = swap(kicks(particles, field), "dom")
    kick_sum = jnp.sum(kick, axis=0).reshape(2, count)
    momentum_out = momentum + kick_scale * kick_sum

    ahead = jnp.where(hist_at == 0, fresh[::-1], incoming)
    history_out = jnp.concatenate([ahead, history[: lags - STEPS]], axis=0)
    return momentum_out, history_out


def solution(mesh):
    everyone = ("hist", "rows", "dom")
    in_specs = (
        P(None, everyone),
        P(None, everyone),
        P(None, everyone),
        P(everyone),
        P(None, everyone),
        P("hist", "rows", None),
        P("hist", "dom", None),
        P("hist", "rows", None, None),
    )
    out_specs = (P(None, everyone), P("hist", "rows", None))
    return jax.shard_map(local, mesh=mesh, in_specs=in_specs, out_specs=out_specs, check_vma=False)
```

time: 439 us -> 159 us (0.36)
  waiting for transfers between devices: 115 us -> 30.8 us
  starting transfers between devices: 113 us -> 29.6 us
  blocking collectives: 131 us -> 75.7 us
  local copies, waits for them, and re-layouts: 36.9 us -> 6.41 us
  matrix products: 26.5 us -> 0 us
  Pallas kernels: 0 us -> 11.8 us
  other arithmetic: 12.9 us -> 2.76 us
    psum x1 -> x0, blocking collectives: 131 us -> none  [local(): whole_grid = lax.psum(partial_grid, ('hist', 'rows', 'dom'))]
    all_to_all x0 -> x4, blocking collectives: none -> 75.7 us  [swap(): return lax.all_to_all(array, axes, split_axis=0, concat_axis=0, tiled=True)]
    all_to_all x12 -> x4, starting transfers between devices: 99.5 us -> 26.1 us  [swap(): return lax.all_to_all(array, axes, split_axis=0, concat_axis=0, tiled=True)]
    all_to_all x12 -> x4, waiting for transfers between devices: 103 us -> 30.8 us  [swap(): return lax.all_to_all(array, axes, split_axis=0, concat_axis=0, tiled=True)]
    dot_general x12 -> x0, matrix products: 26.5 us -> none  [the longest x4 11.1 us: local(): lax.dot_general(row_charged, col_table, contract_first, preferred_element...]
    pallas_call x0 -> x4, Pallas kernels: none -> 11.8 us  [the longest x1 6.16 us: kicks(): pl.pallas_call(kick_kernel, grid=(sources,), in_specs=[pl.BlockSpec((1, l...]
    ppermute x4 -> x1, waiting for transfers between devices: 11.6 us -> 0.01 us  [local(): lax.ppermute(history[lags - STEPS:], 'hist', [(i, i + 1) for i in range(h...]
    ppermute x4 -> x1, starting transfers between devices: 13.7 us -> 3.5 us  [local(): lax.ppermute(history[lags - STEPS:], 'hist', [(i, i + 1) for i in range(h...]
  transfers between devices with their start and end apart: 16 -> 5, of which waited for: 13 -> 4; matrix products, arithmetic and copies ran while one was open for 14% -> 2% of each run, Pallas kernels for 0% -> 0%
where the time goes in v1:
time: 159 us; the launch traced here: 158 us
  blocking collectives  75.7 us (48%)
  waiting for transfers between devices  30.8 us (19%)
  starting transfers between devices  29.6 us (19%)
  Pallas kernels  11.8 us (7%)
  local copies, waits for them, and re-layouts  6.41 us (4%)
  other arithmetic  2.76 us (2%)
    all_to_all x4, blocking collectives, swap(): return lax.all_to_all(array, axes, split_axis=0, concat_axis=0, tiled=True)  75.7 us
    all_to_all x4, waiting for transfers between devices, swap(): return lax.all_to_all(array, axes, split_axis=0, concat_axis=0, tiled=True)  30.8 us
    all_to_all x4, starting transfers between devices, swap(): return lax.all_to_all(array, axes, split_axis=0, concat_axis=0, tiled=True)  26.1 us
    pallas_call x1, Pallas kernels, kicks(): pl.pallas_call(kick_kernel, grid=(sources,), in_specs=[pl.BlockSpec((1, l...  6.16 us
    pallas_call x1, Pallas kernels, deposit(): pl.pallas_call(deposit_kernel, grid=(sources,), in_specs=[pl.BlockSpec((1...  4.05 us
    unnamed x14, local copies, waits for them, and re-layouts  3.55 us
    ppermute x1, starting transfers between devices, local(): lax.ppermute(history[lags - STEPS:], 'hist', [(i, i + 1) for i in range(h...  3.5 us
  transfers between devices with their start and end apart: 5, of which 4 were waited for; matrix products, arithmetic and copies ran while one was open for 2% of the time, Pallas kernels for 0%

profile of v1, /device:TPU:1, one launch (start us, length us, event | category | flops | bytes accessed | tf_op | source)
XLA Modules:
  0.0 157.8 jit_solution(7969264459487568986)
XLA Ops:
  0.6 0.0 copy-start.2
  0.6 0.7 convert_bitcast_fusion
  1.4 0.0 copy-done.2
  1.4 0.0 copy-start.3
  1.4 0.7 copy-done.3
  2.1 0.0 copy-start.5
  2.1 0.7 copy-done.5
  2.8 8.9 %all_to_all.40.particles = f32[4,32,128]{2,1,0:T(8,128)S(1)} all-to-all(f32[4,32,128]{2,1,0:T(8,128)S(1)} %maximum_bitcast_fusion), channel_id=1, replica_groups=mesh['hist'=8,'rows'=8,'dom'=4] {'dom'}, dimensions={0} | all-to-all | bytes 131072 | tf_op jit(solution)/shard_map/all_to_all | solution.py:19
  11.7 4.0 %deposit.1 = bf16[8,64,512]{2,1,0:T(8,128)(2,1)S(1)} custom-call(f32[4,32,128]{2,1,0:T(8,128)S(1)} %all_to_all.40.particles), custom_call_target="tpu_custom_call" | custom-call | tf_op jit(solution)/shard_map/deposit/pallas_call | solution.py:69
  15.7 14.5 %all_to_all.41 = bf16[8,64,512]{2,1,0:T(8,128)(2,1)S(1)} all-to-all(bf16[8,64,512]{2,1,0:T(8,128)(2,1)S(1)} %deposit.1), channel_id=1, replica_groups=mesh['hist'=8,'rows'=8,'dom'=4] {'rows'}, dimensions={0} | all-to-all | bytes 1048576 | tf_op jit(solution)/shard_map/all_to_all | solution.py:19
  30.2 0.1 reduce_sum.57
  30.3 0.8 broadcast_in_dim.22
  31.1 0.0 copy-start.1
  31.1 8.3 %all-to-all-start.2 = ((bf16[8,64,512]{2,1,0:T(8,128)(2,1)}), bf16[8,64,512]{2,1,0:T(8,128)(2,1)S(1)}, u32[]{:S(2)}, u32[]{:S(2)}) async-start(bf16[8,64,512]{2,1,0:T(8,128)(2,1)} %broadcast_in_dim.22), calls=%async_computation.2 | async-start | bytes 1048576 | tf_op jit(solution)/shard_map/all_to_all | solution.py:19
  39.4 0.0 copy-done.1
  39.4 0.0 copy-start
  39.5 3.5 %collective-permute-start = (bf16[4,64,512]{2,1,0:T(8,128)(2,1)S(1)}, bf16[4,64,512]{2,1,0:T(8,128)(2,1)S(1)}, u32[]{:S(2)}, u32[]{:S(2)}) collective-permute-start(bf16[4,64,512]{2,1,0:T(8,128)(2,1)S(1)} %get-tuple-element.3), channel_id=1, source_target_pairs={{0,32},{32,64},{64,96},{96,128},{128,160},{160,192},{192,224},{1,3... | collective-permute-start | bytes 786440 | tf_op jit(solution)/shard_map/ppermute | solution.py:186
  43.0 10.8 %all-to-all-done.2 = bf16[8,64,512]{2,1,0:T(8,128)(2,1)S(1)} async-done(((bf16[8,64,512]{2,1,0:T(8,128)(2,1)}), bf16[8,64,512]{2,1,0:T(8,128)(2,1)S(1)}, u32[]{:S(2)}, u32[]{:S(2)}) %all-to-all-start.2) | async-done | bytes 524320 | tf_op jit(solution)/shard_map/all_to_all | solution.py:19
  53.8 0.1 reduce_sum.58
  53.9 0.7 broadcast_in_dim.23
  54.6 9.4 %all-to-all-start.3 = ((bf16[4,64,512]{2,1,0:T(8,128)(2,1)}), bf16[4,64,512]{2,1,0:T(8,128)(2,1)S(1)}, u32[]{:S(2)}, u32[]{:S(2)}) async-start(bf16[4,64,512]{2,1,0:T(8,128)(2,1)} %broadcast_in_dim.23), calls=%async_computation.3 | async-start | bytes 524288 | tf_op jit(solution)/shard_map/all_to_all | solution.py:19
  64.0 0.0 copy-done
  64.0 0.5 old_mixed.1.mixed_old
  64.6 1.5 copy.19
  66.1 0.0 collective-permute-done.incoming
  66.1 3.1 %all-to-all-done.3.fresh = bf16[4,64,512]{2,1,0:T(8,128)(2,1)S(1)} async-done(((bf16[4,64,512]{2,1,0:T(8,128)(2,1)}), bf16[4,64,512]{2,1,0:T(8,128)(2,1)S(1)}, u32[]{:S(2)}, u32[]{:S(2)}) %all-to-all-start.3) | async-done | bytes 262176 | tf_op jit(solution)/shard_map/all_to_all | solution.py:19
  69.2 1.1 field_parts.1
  70.2 20.7 %all_to_all.42 = bf16[32,16,1024]{2,1,0:T(8,128)(2,1)S(1)} all-to-all(bf16[32,16,1024]{2,1,0:T(8,128)(2,1)S(1)} %field_parts.1), channel_id=1, replica_groups=mesh['hist'=8,'rows'=8,'dom'=4] {'rows','dom'}, dimensions={0} | all-to-all | bytes 2097152 | tf_op jit(solution)/shard_map/all_to_all | solution.py:19
  90.9 0.2 bitcast_reduce_fusion
  91.1 0.1 broadcast_in_dim.24
  91.2 31.6 %all_to_all.43 = bf16[8,64,1024]{2,1,0:T(8,128)(2,1)S(1)} all-to-all(bf16[8,64,1024]{2,1,0:T(8,128)(2,1)S(1)} %broadcast_in_dim.24), channel_id=1, replica_groups=mesh['hist'=8,'rows'=8,'dom'=4] {'hist'}, dimensions={0} | all-to-all | bytes 2097152 | tf_op jit(solution)/shard_map/all_to_all | solution.py:19
  122.9 0.2 reduce_sum.60
  123.0 1.1 broadcast_in_dim.25
  124.1 3.6 %all-to-all-start.6 = ((bf16[8,64,1024]{2,1,0:T(8,128)(2,1)}), bf16[8,64,1024]{2,1,0:T(8,128)(2,1)S(1)}, u32[]{:S(2)}, u32[]{:S(2)}) async-start(bf16[8,64,1024]{2,1,0:T(8,128)(2,1)} %broadcast_in_dim.25), calls=%async_computation.6 | async-start | bytes 2097152 | tf_op jit(solution)/shard_map/all_to_all | solution.py:19
  127.7 0.1 reverse_select_fusion
  127.8 14.6 %all-to-all-done.6 = bf16[8,64,1024]{2,1,0:T(8,128)(2,1)S(1)} async-done(((bf16[8,64,1024]{2,1,0:T(8,128)(2,1)}), bf16[8,64,1024]{2,1,0:T(8,128)(2,1)S(1)}, u32[]{:S(2)}, u32[]{:S(2)}) %all-to-all-start.6) | async-done | bytes 1048608 | tf_op jit(solution)/shard_map/all_to_all | solution.py:19
  142.3 6.2 %kicks.1 = f32[4,16,128]{2,1,0:T(8,128)} custom-call(f32[4,32,128]{2,1,0:T(8,128)S(1)} %all_to_all.40.particles, bf16[512,1024]{1,0:T(8,128)(2,1)S(1)} %bitcast.39), custom_call_target="tpu_custom_call" | custom-call | tf_op jit(solution)/shard_map/kicks/pallas_call | solution.py:98
  148.5 4.8 %all-to-all-start.7 = ((f32[4,16,128]{2,1,0:T(8,128)}), f32[4,16,128]{2,1,0:T(8,128)S(1)}, u32[]{:S(2)}, u32[]{:S(2)}) async-start(f32[4,16,128]{2,1,0:T(8,128)} %kicks.1), calls=%async_computation.7 | async-start | bytes 65536 | tf_op jit(solution)/shard_map/all_to_all | solution.py:19
  153.4 0.8 pad_maximum_fusion
  154.2 2.3 %all-to-all-done.7 = f32[4,16,128]{2,1,0:T(8,128)S(1)} async-done(((f32[4,16,128]{2,1,0:T(8,128)}), f32[4,16,128]{2,1,0:T(8,128)S(1)}, u32[]{:S(2)}, u32[]{:S(2)}) %all-to-all-start.7) | async-done | bytes 32800 | tf_op jit(solution)/shard_map/all_to_all | solution.py:19
  156.5 0.0 copy-start.4
  156.6 0.7 copy-done.4
  157.2 0.6 add.3
  (12 shorter events, 0.1 us)
Async XLA Ops:
  0.6 0.7 copy-start.2
  1.4 0.7 copy-start.3
  2.1 0.7 copy-start.5
  31.1 8.3 %copy-start.1 = (bf16[8,64,512]{2,1,0:T(8,128)(2,1)S(1)}, bf16[8,64,512]{2,1,0:T(8,128)(2,1)}, u32[]{:S(2)}) copy-start(bf16[8,64,512]{2,1,0:T(8,128)(2,1)} %history.1) | copy-start | bytes 1572868
  31.1 22.7 %all-to-all-start.2 = ((bf16[8,64,512]{2,1,0:T(8,128)(2,1)}), bf16[8,64,512]{2,1,0:T(8,128)(2,1)S(1)}, u32[]{:S(2)}, u32[]{:S(2)}) async-start(bf16[8,64,512]{2,1,0:T(8,128)(2,1)} %broadcast_in_dim.22), calls=%async_computation.2 | async-start | bytes 1048576 | tf_op jit(solution)/shard_map/all_to_all | solution.py:19
  39.4 24.6 %copy-start = (bf16[8,128,512]{2,1,0:T(8,128)(2,1)S(1)}, bf16[8,128,512]{2,1,0:T(8,128)(2,1)}, u32[]{:S(2)}) copy-start(bf16[8,128,512]{2,1,0:T(8,128)(2,1)} %cols.1) | copy-start | bytes 3145732
  39.5 26.6 %collective-permute-start = (bf16[4,64,512]{2,1,0:T(8,128)(2,1)S(1)}, bf16[4,64,512]{2,1,0:T(8,128)(2,1)S(1)}, u32[]{:S(2)}, u32[]{:S(2)}) collective-permute-start(bf16[4,64,512]{2,1,0:T(8,128)(2,1)S(1)} %get-tuple-element.3), channel_id=1, source_target_pairs={{0,32},{32,64},{64,96},{96,128},{128,160},{160,192},{192,224},{1,3... | collective-permute-start | bytes 786440 | tf_op jit(solution)/shard_map/ppermute | solution.py:186
  54.6 14.6 %all-to-all-start.3 = ((bf16[4,64,512]{2,1,0:T(8,128)(2,1)}), bf16[4,64,512]{2,1,0:T(8,128)(2,1)S(1)}, u32[]{:S(2)}, u32[]{:S(2)}) async-start(bf16[4,64,512]{2,1,0:T(8,128)(2,1)} %broadcast_in_dim.23), calls=%async_computation.3 | async-start | bytes 524288 | tf_op jit(solution)/shard_map/all_to_all | solution.py:19
  124.1 18.2 %all-to-all-start.6 = ((bf16[8,64,1024]{2,1,0:T(8,128)(2,1)}), bf16[8,64,1024]{2,1,0:T(8,128)(2,1)S(1)}, u32[]{:S(2)}, u32[]{:S(2)}) async-start(bf16[8,64,1024]{2,1,0:T(8,128)(2,1)} %broadcast_in_dim.25), calls=%async_computation.6 | async-start | bytes 2097152 | tf_op jit(solution)/shard_map/all_to_all | solution.py:19
  148.5 8.0 %all-to-all-start.7 = ((f32[4,16,128]{2,1,0:T(8,128)}), f32[4,16,128]{2,1,0:T(8,128)S(1)}, u32[]{:S(2)}, u32[]{:S(2)}) async-start(f32[4,16,128]{2,1,0:T(8,128)} %kicks.1), calls=%async_computation.7 | async-start | bytes 65536 | tf_op jit(solution)/shard_map/all_to_all | solution.py:19
  156.5 0.7 copy-start.4

commit v2 on v1

v2 whole, which is shorter than its diff:
```python
import functools

import jax
import jax.numpy as jnp
from jax import lax
from jax.experimental import pallas as pl
from jax.experimental.pallas import tpu as pltpu
from jax.sharding import PartitionSpec as P

NG = 512
BINS = 16
STEPS = 4
LANES = 128

kick_scale = 0.5
f32 = jnp.float32
bf16 = jnp.bfloat16


def swap(array, axes):
    return lax.all_to_all(array, axes, split_axis=0, concat_axis=0, tiled=True)


def to_all(array, axes):
    copies = jnp.broadcast_to(array, (lax.axis_size(axes), *array.shape))
    return swap(copies, axes)


def hat(places, cell, fraction):
    return jnp.maximum(1.0 - jnp.abs((places - cell) - fraction), jnp.zeros((), bf16))


def window(cell, first):
    return jnp.clip(cell - first, -2.0, 258.0).astype(bf16)


def unpack(particles, source):
    lines = particles.shape[1] // 4

    def field(which):
        rows = [particles[source, which * lines + k : which * lines + k + 1, :] for k in range(lines)]
        return jnp.concatenate(rows, axis=1)

    bins = field(2)
    row_bin = jnp.floor(bins * (1.0 / BINS))
    col_bin = bins - row_bin * BINS
    row_fraction = ((row_bin + 0.5) * (1.0 / BINS)).astype(bf16)
    col_fraction = ((col_bin + 0.5) * (1.0 / BINS)).astype(bf16)
    return field(0), row_fraction, field(1), col_fraction, field(3)


def lines_of(count, size):
    return lax.broadcasted_iota(jnp.int32, (count, size), 0)


def deposit_kernel(lines, band, parts, half, particles, out):
    sources, fields, _ = particles.shape
    bands, share = lines // band, band // parts
    places = lines_of(lines, fields // 4 * LANES).astype(f32).astype(bf16)
    total = None
    for source in range(sources):
        row, row_fraction, col, col_fraction, charge = unpack(particles, source)
        row_table = hat(places, window(row, (half[0] * lines).astype(f32)), row_fraction) * charge.astype(bf16)
        col_tables = [hat(places, window(col, float(first)), col_fraction) for first in range(0, NG, lines)]
        col_table = jnp.concatenate(col_tables, axis=0)
        part = lax.dot_general(row_table, col_table, (((1,), (1,)), ((), ())), preferred_element_type=f32)
        total = part if total is None else total + part
    grid = total.astype(bf16)
    for n in range(bands * parts):
        part, at = divmod(n, bands)
        first = at * band + part * share
        out[n] = grid[first : first + share]


def deposit(half, particles, lines, band, parts):
    blocks = (lines // band * parts, band // parts, NG)
    vmem = pl.BlockSpec(memory_space=pltpu.VMEM)
    return pl.pallas_call(
        functools.partial(deposit_kernel, lines, band, parts),
        in_specs=[pl.BlockSpec(memory_space=pltpu.SMEM), vmem],
        out_specs=vmem,
        out_shape=jax.ShapeDtypeStruct(blocks, bf16),
        compiler_params=pltpu.CompilerParams(vmem_limit_bytes=48 << 20),
        name="deposit",
    )(half, particles)


def kick_kernel(half, particles, field, out):
    sources, fields, _ = particles.shape
    width = field.shape[0]
    lines = fields // 4
    places = lines_of(width, lines * LANES)
    row_places = places.astype(f32).astype(bf16)
    column = (((places >> 4) & 3) * 128 + (places >> 6) * 16 + (places & 15)).astype(f32)

    def tables(source):
        row, row_fraction, col, col_fraction, _ = unpack(particles, source)
        row_tables = [hat(row_places, window(row, float(first)), row_fraction) for first in range(0, NG, width)]
        at_col = col + col_fraction.astype(f32) - (half[0] * 64).astype(f32)
        return jnp.concatenate(row_tables, axis=0), jnp.maximum(1.0 - jnp.abs(column - at_col), 0.0)

    ready = tables(0)
    for source in range(sources):
        row_table, col_table = ready
        if source + 1 < sources:
            ready = tables(source + 1)
        for comp in range(2):
            along = jnp.dot(field[:, comp * NG : (comp + 1) * NG], row_table, preferred_element_type=f32)
            kick = jnp.sum(along * col_table, axis=0, keepdims=True)
            for k in range(lines):
                out[source, comp * lines + k : comp * lines + k + 1, :] = kick[:, k * LANES : (k + 1) * LANES]


def kicks(half, particles, field):
    sources, fields, _ = particles.shape
    vmem = pl.BlockSpec(memory_space=pltpu.VMEM)
    return pl.pallas_call(
        kick_kernel,
        in_specs=[pl.BlockSpec(memory_space=pltpu.SMEM), vmem, vmem],
        out_specs=vmem,
        out_shape=jax.ShapeDtypeStruct((sources, fields // 2, LANES), f32),
        compiler_params=pltpu.CompilerParams(vmem_limit_bytes=48 << 20),
        name="kicks",
    )(half, particles, field)


def old_mixed_kernel(history, cols, out):
    lags, band, _ = history.shape
    for lag in range(1, lags):
        steps = min(lag, STEPS)
        grids = history[lag - steps : lag].reshape(steps * band, NG)
        mixed = lax.dot_general(grids, cols[lag], (((1,), (1,)), ((), ())), preferred_element_type=f32)
        mixed = mixed.astype(bf16).reshape(steps, band, mixed.shape[1])
        for step in range(steps):
            out[step, lag] = mixed[steps - 1 - step]
    for step in range(STEPS):
        for lag in range(step + 1):
            out[step, lag] = jnp.zeros(out.shape[2:], bf16)


def old_mixed(history, cols):
    lags, band, _ = history.shape
    return pl.pallas_call(
        old_mixed_kernel,
        out_shape=jax.ShapeDtypeStruct((STEPS, lags, band, cols.shape[1]), bf16),
        compiler_params=pltpu.CompilerParams(vmem_limit_bytes=48 << 20),
        name="old_mixed",
    )(history, cols)


def field_kernel(first, fresh, incoming, cols, rows, mixed_old, out, newer):
    band = incoming.shape[1]
    parts_in = fresh.shape[0] // STEPS
    ahead = []
    for n in range(STEPS):
        density = [fresh[part * STEPS + STEPS - 1 - n] for part in range(parts_in)]
        ahead.append(jnp.where(first[0] == 1, jnp.concatenate(density, axis=0), incoming[n]))
        newer[n] = ahead[n]
    grids = jnp.concatenate(ahead, axis=0)
    wide = cols.shape[1]
    parts = [[] for _ in range(STEPS)]
    for lag in range(STEPS):
        count = STEPS - lag
        mixed = lax.dot_general(
            grids[lag * band :], cols[lag], (((1,), (1,)), ((), ())), preferred_element_type=f32
        ).astype(bf16)
        for n in range(count):
            parts[STEPS - 1 - n].append(mixed[n * band : (n + 1) * band])
    bands = out.shape[0] // STEPS
    share = wide // bands
    for step in range(STEPS):
        lines = parts[step] + [mixed_old[step, lag] for lag in range(step + 1, mixed_old.shape[1])]
        lhs = jnp.concatenate(lines, axis=0)
        field = lax.dot_general(lhs, rows[...], (((0,), (0,)), ((), ())), preferred_element_type=f32)
        field = field.astype(bf16)
        for band_to in range(bands):
            out[band_to * STEPS + step] = field[band_to * share : (band_to + 1) * share]


def field_parts(first, fresh, incoming, cols, rows, mixed_old, bands):
    wide = cols.shape[1]
    vmem = pl.BlockSpec(memory_space=pltpu.VMEM)
    return pl.pallas_call(
        field_kernel,
        in_specs=[pl.BlockSpec(memory_space=pltpu.SMEM)] + [vmem] * 5,
        out_specs=(vmem, vmem),
        out_shape=(
            jax.ShapeDtypeStruct((bands * STEPS, wide // bands, rows.shape[1]), bf16),
            jax.ShapeDtypeStruct(incoming.shape, bf16),
        ),
        compiler_params=pltpu.CompilerParams(vmem_limit_bytes=48 << 20),
        name="field_parts",
    )(first, fresh, incoming, cols, rows, mixed_old)


def local(row_index, col_index, bin_index, charge, momentum, history, kernel_cols, kernel_rows):
    lags, band, _ = history.shape
    count = charge.shape[0]
    bands = NG // band
    lines = count // LANES
    hist_at = lax.axis_index("hist")
    hist_size = lax.axis_size("hist")

    fields = [row_index.astype(f32), col_index.astype(f32), bin_index.astype(f32)]
    fields.append(jnp.broadcast_to(charge.astype(f32), (STEPS, count)))
    packed = jnp.stack([x.reshape(STEPS, lines, LANES) for x in fields], axis=1)
    packed = jnp.broadcast_to(packed.reshape(STEPS, 4 * lines, LANES), (2, STEPS, 4 * lines, LANES))
    particles = swap(packed.reshape(2 * STEPS, 4 * lines, LANES), ("xh", "dom"))
    half = lax.axis_index("xh").reshape(1)

    incoming = lax.ppermute(history[lags - STEPS :], "hist", [(i, i + 1) for i in range(hist_size - 1)])
    mixed_old = old_mixed(history, kernel_cols)
    rows_flat = kernel_rows.reshape(lags * band, 2 * NG)

    grid = deposit(half, particles, NG // 2, band, hist_size)
    grid, incoming = lax.optimization_barrier((grid, incoming))
    density = jnp.sum(swap(grid, ("hist", "y")).astype(f32), axis=0).astype(bf16)
    fresh = to_all(density, ("hist", "dom"))

    first = (hist_at == 0).astype(jnp.int32).reshape(1)
    partial, ahead = field_parts(first, fresh, incoming, kernel_cols[:STEPS], rows_flat, mixed_old, bands)
    received = swap(partial, ("xh", "y", "dom"))
    share = received.shape[1]
    by_column = jnp.sum(received.reshape(bands, STEPS * share, 2 * NG).astype(f32), axis=0)
    by_column = by_column.reshape(hist_size, -1, 2 * NG)
    summed = jnp.sum(swap(by_column, "hist"), axis=0).astype(bf16)
    whole = to_all(summed, "hist").reshape(STEPS * share, 2 * NG)
    field = to_all(whole, "y").reshape(NG // 2, 2 * NG)

    kick = swap(kicks(half, particles, field), ("xh", "dom"))
    kick_sum = jnp.sum(kick, axis=0).reshape(2, count)
    momentum_out = momentum + kick_scale * kick_sum

    history_out = jnp.concatenate([ahead, history[: lags - STEPS]], axis=0)
    return momentum_out, history_out


def solution(mesh):
    split = {"hist": ("hist",), "rows": ("xh", "y"), "dom": ("dom",)}
    sizes = [mesh.shape["hist"], 2, mesh.shape["rows"] // 2, mesh.shape["dom"]]
    fine = jax.sharding.Mesh(mesh.devices.reshape(sizes), ("hist", "xh", "y", "dom"))

    def spec(*dims):
        return P(*[None if dim is None else tuple(a for name in dim for a in split[name]) for dim in dims])

    everyone = ("hist", "rows", "dom")
    in_specs = (
        spec(None, everyone),
        spec(None, everyone),
        spec(None, everyone),
        spec(everyone),
        spec(None, everyone),
        spec(["hist"], ["rows"], None),
        spec(["hist"], ["dom"], None),
        spec(["hist"], ["rows"], None, None),
    )
    out_specs = (spec(None, everyone), spec(["hist"], ["rows"], None))
    return jax.shard_map(local, mesh=fine, in_specs=in_specs, out_specs=out_specs, check_vma=False)
```

time: 159 us -> 136 us (0.86)
  waiting for transfers between devices: 30.8 us -> 18.7 us
  starting transfers between devices: 29.6 us -> 21.7 us
  blocking collectives: 75.7 us -> 78.5 us
  local copies, waits for them, and re-layouts: 6.41 us -> 4.09 us
  Pallas kernels: 11.8 us -> 10.1 us
    all_to_all x4 -> x3, waiting for transfers between devices: 30.8 us -> 18.7 us  [swap(): return lax.all_to_all(array, axes, split_axis=0, concat_axis=0, tiled=True)]
    all_to_all x4 -> x3, starting transfers between devices: 26.1 us -> 17.3 us  [swap(): return lax.all_to_all(array, axes, split_axis=0, concat_axis=0, tiled=True)]
    all_to_all x4 -> x5, blocking collectives: 75.7 us -> 78.5 us  [swap(): return lax.all_to_all(array, axes, split_axis=0, concat_axis=0, tiled=True)]
    unnamed x14 -> x16, local copies, waits for them, and re-layouts: 3.55 us -> 1.5 us
    broadcast_in_dim x4 -> x3, local copies, waits for them, and re-layouts: 2.77 us -> 0.78 us  [to_all(): copies = jnp.broadcast_to(array, (lax.axis_size(axes), *array.shape))]
    pallas_call x2, Pallas kernels: 10.2 us -> 8.47 us  [the longest x1 5.64 us: kicks(): pl.pallas_call(kick_kernel, in_specs=[pl.BlockSpec(memory_space=pltpu.SME...]
  transfers between devices with their start and end apart: 5 -> 4, of which waited for: 4 -> 3; matrix products, arithmetic and copies ran while one was open for 2% -> 2% of each run, Pallas kernels for 0% -> 2%
where the time goes in v2:
time: 136 us
  blocking collectives  78.5 us (58%)
  starting transfers between devices  21.7 us (16%)
  waiting for transfers between devices  18.7 us (14%)
  Pallas kernels  10.1 us (7%)
  local copies, waits for them, and re-layouts  4.09 us (3%)
  other arithmetic  1.73 us (1%)
    all_to_all x5, blocking collectives, swap(): return lax.all_to_all(array, axes, split_axis=0, concat_axis=0, tiled=True)  78.5 us
    all_to_all x3, waiting for transfers between devices, swap(): return lax.all_to_all(array, axes, split_axis=0, concat_axis=0, tiled=True)  18.7 us
    all_to_all x3, starting transfers between devices, swap(): return lax.all_to_all(array, axes, split_axis=0, concat_axis=0, tiled=True)  17.3 us
    pallas_call x1, Pallas kernels, kicks(): pl.pallas_call(kick_kernel, in_specs=[pl.BlockSpec(memory_space=pltpu.SME...  5.64 us
    ppermute x1, starting transfers between devices, local(): lax.ppermute(history[lags - STEPS:], 'hist', [(i, i + 1) for i in range(h...  4.39 us
    pallas_call x1, Pallas kernels, deposit(): pl.pallas_call(functools.partial(deposit_kernel, lines, band, parts), in_...  2.84 us
  transfers between devices with their start and end apart: 4, of which 3 were waited for; matrix products, arithmetic and copies ran while one was open for 2% of the time, Pallas kernels for 2%

profile of v2, /device:TPU:1, one launch (start us, length us, event | category | flops | bytes accessed | tf_op | source)
XLA Modules:
  0.0 135.7 jit_solution(540492572573064855)
XLA Ops:
  0.6 0.0 copy-start.2
  0.6 0.0 copy-start.3
  0.7 0.0 copy-start.4
  0.7 0.0 copy-start.6
  0.7 1.1 fusion
  1.8 4.4 %collective-permute-start = (bf16[4,64,512]{2,1,0:T(8,128)(2,1)S(1)}, bf16[4,64,512]{2,1,0:T(8,128)(2,1)S(1)}, u32[]{:S(2)}, u32[]{:S(2)}) collective-permute-start(bf16[4,64,512]{2,1,0:T(8,128)(2,1)S(1)} %get-tuple-element.11), channel_id=1, source_target_pairs={{0,32},{32,64},{64,96},{96,128},{128,160},{160,192},{192,224},{1,3... | collective-permute-start | bytes 786440 | tf_op jit(solution)/shard_map/ppermute | solution.py:211
  6.2 0.0 copy-done.2
  6.2 0.0 copy-done.3
  6.2 0.0 copy-done.4
  6.2 0.0 copy-done.6
  6.3 0.7 broadcast_in_dim.22
  7.0 5.3 %all-to-all-start = ((f32[8,32,128]{2,1,0:T(8,128)}), f32[8,32,128]{2,1,0:T(8,128)S(1)}, u32[]{:S(2)}, u32[]{:S(2)}) async-start(f32[8,32,128]{2,1,0:T(8,128)} %bitcast.3), calls=%async_computation | async-start | bytes 262144 | tf_op jit(solution)/shard_map/all_to_all | solution.py:21
  12.2 0.0 copy-start
  12.2 0.0 copy-start.1
  12.2 5.3 %all-to-all-done.particles = f32[8,32,128]{2,1,0:T(8,128)S(1)} async-done(((f32[8,32,128]{2,1,0:T(8,128)}), f32[8,32,128]{2,1,0:T(8,128)S(1)}, u32[]{:S(2)}, u32[]{:S(2)}) %all-to-all-start) | async-done | bytes 131104 | tf_op jit(solution)/shard_map/all_to_all | solution.py:21
  17.5 2.8 %deposit.1 = bf16[32,8,512]{2,1,0:T(8,128)(2,1)S(1)} custom-call(s32[1]{0:T(128)} %bitcast.half, f32[8,32,128]{2,1,0:T(8,128)S(1)} %all-to-all-done.particles), custom_call_target="tpu_custom_call" | custom-call | tf_op jit(solution)/shard_map/deposit/pallas_call | solution.py:78
  20.3 0.0 collective-permute-done.incoming
  20.4 21.2 %all_to_all.40 = bf16[32,8,512]{2,1,0:T(8,128)(2,1)S(1)} all-to-all(bf16[32,8,512]{2,1,0:T(8,128)(2,1)S(1)} %deposit.1), channel_id=1, replica_groups=mesh['hist'=8,'xh'=2,'y'=4,'dom'=4] {'hist','y'}, dimensions={0} | all-to-all | bytes 524288 | tf_op jit(solution)/shard_map/all_to_all | solution.py:21
  41.5 0.1 reduce_sum.39
  41.6 0.7 broadcast_in_dim.23
  42.3 6.1 %all-to-all-start.2 = ((bf16[32,8,512]{2,1,0:T(8,128)(2,1)}), bf16[32,8,512]{2,1,0:T(8,128)(2,1)S(1)}, u32[]{:S(2)}, u32[]{:S(2)}) async-start(bf16[32,8,512]{2,1,0:T(8,128)(2,1)} %broadcast_in_dim.23), calls=%async_computation.2 | async-start | bytes 524288 | tf_op jit(solution)/shard_map/all_to_all | solution.py:21
  48.4 0.0 copy-done
  48.4 0.0 copy-done.1
  48.4 0.5 old_mixed.1.mixed_old
  49.0 1.5 %copy.13 = bf16[64,8,2,512]{3,1,2,0:T(8,128)(2,1)S(1)} copy(bf16[64,8,2,512]{3,2,1,0:T(2,128)(2,1)} %bitcast.38) | data formatting | bytes 2097152
  50.5 9.4 %all-to-all-done.2.fresh = bf16[32,8,512]{2,1,0:T(8,128)(2,1)S(1)} async-done(((bf16[32,8,512]{2,1,0:T(8,128)(2,1)}), bf16[32,8,512]{2,1,0:T(8,128)(2,1)S(1)}, u32[]{:S(2)}, u32[]{:S(2)}) %all-to-all-start.2) | async-done | bytes 262176 | tf_op jit(solution)/shard_map/all_to_all | solution.py:21
  59.9 1.1 field_parts.1
  60.9 22.0 %all_to_all.41 = bf16[32,16,1024]{2,1,0:T(8,128)(2,1)S(1)} all-to-all(bf16[32,16,1024]{2,1,0:T(8,128)(2,1)S(1)} %get-tuple-element.8), channel_id=1, replica_groups=mesh['hist'=8,'xh'=2,'y'=4,'dom'=4] {'xh','y','dom'}, dimensions={0} | all-to-all | bytes 2097152 | tf_op jit(solution)/shard_map/all_to_all | solution.py:21
  82.9 0.2 convert_reduce_fusion
  83.1 14.8 %all_to_all.42 = f32[8,8,1024]{2,1,0:T(8,128)S(1)} all-to-all(f32[8,8,1024]{2,1,0:T(8,128)S(1)} %bitcast.37), channel_id=1, replica_groups=mesh['hist'=8,'xh'=2,'y'=4,'dom'=4] {'hist'}, dimensions={0} | all-to-all | bytes 524288 | tf_op jit(solution)/shard_map/all_to_all | solution.py:21
  97.9 10.6 %all_to_all.43 = bf16[8,8,1024]{2,1,0:T(8,128)(2,1)S(1)} all-to-all(bf16[8,8,1024]{2,1,0:T(8,128)(2,1)S(1)} %broadcast_in_dim.24), channel_id=1, replica_groups=mesh['hist'=8,'xh'=2,'y'=4,'dom'=4] {'hist'}, dimensions={0} | all-to-all | bytes 262144 | tf_op jit(solution)/shard_map/all_to_all | solution.py:21
  108.5 10.1 %all_to_all.44 = bf16[4,64,1024]{2,1,0:T(8,128)(2,1)S(1)} all-to-all(bf16[4,64,1024]{2,1,0:T(8,128)(2,1)S(1)} %broadcast_in_dim.25), channel_id=1, replica_groups=mesh['hist'=8,'xh'=2,'y'=4,'dom'=4] {'y'}, dimensions={0} | all-to-all | bytes 1048576 | tf_op jit(solution)/shard_map/all_to_all | solution.py:21
  118.6 0.0 copy-start.5
  118.6 5.6 %kicks.1 = f32[8,16,128]{2,1,0:T(8,128)} custom-call(s32[1]{0:T(128)} %bitcast.half, f32[8,32,128]{2,1,0:T(8,128)S(1)} %all-to-all-done.particles, bf16[256,1024]{1,0:T(8,128)(2,1)S(1)} %bitcast.35), custom_call_target="tpu_custom_call" | custom-call | tf_op jit(solution)/shard_map/kicks/pallas_call | solution.py:117
  124.2 6.0 %all-to-all-start.7 = ((f32[8,16,128]{2,1,0:T(8,128)}), f32[8,16,128]{2,1,0:T(8,128)S(1)}, u32[]{:S(2)}, u32[]{:S(2)}) async-start(f32[8,16,128]{2,1,0:T(8,128)} %kicks.1), calls=%async_computation.7 | async-start | bytes 131072 | tf_op jit(solution)/shard_map/all_to_all | solution.py:21
  130.2 0.8 pad_maximum_fusion
  131.1 4.0 %all-to-all-done.7 = f32[8,16,128]{2,1,0:T(8,128)S(1)} async-done(((f32[8,16,128]{2,1,0:T(8,128)}), f32[8,16,128]{2,1,0:T(8,128)S(1)}, u32[]{:S(2)}, u32[]{:S(2)}) %all-to-all-start.7) | async-done | bytes 65568 | tf_op jit(solution)/shard_map/all_to_all | solution.py:21
  135.1 0.0 copy-done.5
  135.1 0.6 add.3
  (15 shorter events, 0.2 us)
Async XLA Ops:
  0.6 5.5 %copy-start.2 = (s32[4,1024]{1,0:T(4,128)S(1)}, s32[4,1024]{1,0:T(4,128)}, u32[]{:S(2)}) copy-start(s32[4,1024]{1,0:T(4,128)} %param.8) | copy-start | bytes 49156
  0.6 5.6 %copy-start.3 = (s32[4,1024]{1,0:T(4,128)S(1)}, s32[4,1024]{1,0:T(4,128)}, u32[]{:S(2)}) copy-start(s32[4,1024]{1,0:T(4,128)} %param.9) | copy-start | bytes 49156
  0.7 5.6 %copy-start.4 = (s32[4,1024]{1,0:T(4,128)S(1)}, s32[4,1024]{1,0:T(4,128)}, u32[]{:S(2)}) copy-start(s32[4,1024]{1,0:T(4,128)} %param.10) | copy-start | bytes 49156
  0.7 5.6 %copy-start.6 = (bf16[1024]{0:T(1024)(128)(2,1)S(1)}, bf16[1024]{0:T(1024)(128)(2,1)}, u32[]{:S(2)}) copy-start(bf16[1024]{0:T(1024)(128)(2,1)} %param.11) | copy-start | bytes 6148
  1.8 18.6 %collective-permute-start = (bf16[4,64,512]{2,1,0:T(8,128)(2,1)S(1)}, bf16[4,64,512]{2,1,0:T(8,128)(2,1)S(1)}, u32[]{:S(2)}, u32[]{:S(2)}) collective-permute-start(bf16[4,64,512]{2,1,0:T(8,128)(2,1)S(1)} %get-tuple-element.11), channel_id=1, source_target_pairs={{0,32},{32,64},{64,96},{96,128},{128,160},{160,192},{192,224},{1,3... | collective-permute-start | bytes 786440 | tf_op jit(solution)/shard_map/ppermute | solution.py:211
  7.0 10.5 %all-to-all-start = ((f32[8,32,128]{2,1,0:T(8,128)}), f32[8,32,128]{2,1,0:T(8,128)S(1)}, u32[]{:S(2)}, u32[]{:S(2)}) async-start(f32[8,32,128]{2,1,0:T(8,128)} %bitcast.3), calls=%async_computation | async-start | bytes 262144 | tf_op jit(solution)/shard_map/all_to_all | solution.py:21
  12.2 36.2 %copy-start = (bf16[8,128,512]{2,1,0:T(8,128)(2,1)S(1)}, bf16[8,128,512]{2,1,0:T(8,128)(2,1)}, u32[]{:S(2)}) copy-start(bf16[8,128,512]{2,1,0:T(8,128)(2,1)} %cols.1) | copy-start | bytes 3145732
  12.2 36.2 %copy-start.1 = (bf16[8,64,512]{2,1,0:T(8,128)(2,1)S(1)}, bf16[8,64,512]{2,1,0:T(8,128)(2,1)}, u32[]{:S(2)}) copy-start(bf16[8,64,512]{2,1,0:T(8,128)(2,1)} %history.1) | copy-start | bytes 1572868
  42.3 17.6 %all-to-all-start.2 = ((bf16[32,8,512]{2,1,0:T(8,128)(2,1)}), bf16[32,8,512]{2,1,0:T(8,128)(2,1)S(1)}, u32[]{:S(2)}, u32[]{:S(2)}) async-start(bf16[32,8,512]{2,1,0:T(8,128)(2,1)} %broadcast_in_dim.23), calls=%async_computation.2 | async-start | bytes 524288 | tf_op jit(solution)/shard_map/all_to_all | solution.py:21
  118.6 16.6 %copy-start.5 = (f32[2,1024]{1,0:T(2,128)S(1)}, f32[2,1024]{1,0:T(2,128)}, u32[]{:S(2)}) copy-start(f32[2,1024]{1,0:T(2,128)} %param.12) | copy-start | bytes 24580
  124.2 10.9 %all-to-all-start.7 = ((f32[8,16,128]{2,1,0:T(8,128)}), f32[8,16,128]{2,1,0:T(8,128)S(1)}, u32[]{:S(2)}, u32[]{:S(2)}) async-start(f32[8,16,128]{2,1,0:T(8,128)} %kicks.1), calls=%async_computation.7 | async-start | bytes 131072 | tf_op jit(solution)/shard_map/all_to_all | solution.py:21

commit v3 on v2

--- a/solution.py
+++ b/solution.py
@@ -35,11 +35,8 @@
 
 
 def unpack(particles, source):
-    lines = particles.shape[1] // 4
-
     def field(which):
-        rows = [particles[source, which * lines + k : which * lines + k + 1, :] for k in range(lines)]
-        return jnp.concatenate(rows, axis=1)
+        return particles[source, which : which + 1, :]
 
     bins = field(2)
     row_bin = jnp.floor(bins * (1.0 / BINS))
@@ -53,10 +50,33 @@
     return lax.broadcasted_iota(jnp.int32, (count, size), 0)
 
 
+def pack_kernel(row, col, bins, charge, out):
+    steps, count = row.shape
+    weight = charge[...].astype(f32).reshape(1, count)
+    halves = out.shape[0] // steps
+    for step in range(steps):
+        fields = [ref[step : step + 1, :].astype(f32) for ref in (row, col, bins)]
+        packed = jnp.concatenate(fields + [weight], axis=0)
+        for half in range(halves):
+            out[step * halves + half] = packed
+
+
+def pack(row, col, bins, charge, halves):
+    steps, count = row.shape
+    vmem = pl.BlockSpec(memory_space=pltpu.VMEM)
+    return pl.pallas_call(
+        pack_kernel,
+        in_specs=[vmem] * 4,
+        out_specs=vmem,
+        out_shape=jax.ShapeDtypeStruct((halves * steps, 4, count), f32),
+        name="pack",
+    )(row, col, bins, charge)
+
+
 def deposit_kernel(lines, band, parts, half, particles, out):
-    sources, fields, _ = particles.shape
+    sources, _, count = particles.shape
     bands, share = lines // band, band // parts
-    places = lines_of(lines, fields // 4 * LANES).astype(f32).astype(bf16)
+    places = lines_of(lines, count).astype(f32).astype(bf16)
     total = None
     for source in range(sources):
         row, row_fraction, col, col_fraction, charge = unpack(particles, source)
@@ -67,7 +87,7 @@
         total = part if total is None else total + part
     grid = total.astype(bf16)
     for n in range(bands * parts):
-        part, at = divmod(n, bands)
+        at, part = divmod(n, parts)
         first = at * band + part * share
         out[n] = grid[first : first + share]
 
@@ -81,17 +101,19 @@
         out_specs=vmem,
         out_shape=jax.ShapeDtypeStruct(blocks, bf16),
         compiler_params=pltpu.CompilerParams(vmem_limit_bytes=48 << 20),
+        cost_estimate=pl.CostEstimate(flops=4 * NG * NG * 4096, transcendentals=0, bytes_accessed=1 << 20),
         name="deposit",
     )(half, particles)
 
 
 def kick_kernel(half, particles, field, out):
-    sources, fields, _ = particles.shape
+    sources, _, count = particles.shape
     width = field.shape[0]
-    lines = fields // 4
-    places = lines_of(width, lines * LANES)
+    lines = count // LANES
+    places = lines_of(width, count)
     row_places = places.astype(f32).astype(bf16)
-    column = (((places >> 4) & 3) * 128 + (places >> 6) * 16 + (places & 15)).astype(f32)
+    column = ((places >> 4) & 3) * 128 + (places >> 6) * 16 + (places & 15)
+    column = column.astype(f32)
 
     def tables(source):
         row, row_fraction, col, col_fraction, _ = unpack(particles, source)
@@ -112,19 +134,19 @@
 
 
 def kicks(half, particles, field):
-    sources, fields, _ = particles.shape
+    sources, _, count = particles.shape
     vmem = pl.BlockSpec(memory_space=pltpu.VMEM)
     return pl.pallas_call(
         kick_kernel,
         in_specs=[pl.BlockSpec(memory_space=pltpu.SMEM), vmem, vmem],
         out_specs=vmem,
-        out_shape=jax.ShapeDtypeStruct((sources, fields // 2, LANES), f32),
+        out_shape=jax.ShapeDtypeStruct((sources, 2 * count // LANES, LANES), f32),
         compiler_params=pltpu.CompilerParams(vmem_limit_bytes=48 << 20),
         name="kicks",
     )(half, particles, field)
 
 
-def old_mixed_kernel(history, cols, out):
+def old_mixed_kernel(history, cols, out, kept):
     lags, band, _ = history.shape
     for lag in range(1, lags):
         steps = min(lag, STEPS)
@@ -136,25 +158,30 @@
     for step in range(STEPS):
         for lag in range(step + 1):
             out[step, lag] = jnp.zeros(out.shape[2:], bf16)
+    kept[...] = history[: lags - STEPS]
 
 
 def old_mixed(history, cols):
     lags, band, _ = history.shape
     return pl.pallas_call(
         old_mixed_kernel,
-        out_shape=jax.ShapeDtypeStruct((STEPS, lags, band, cols.shape[1]), bf16),
+        out_shape=(
+            jax.ShapeDtypeStruct((STEPS, lags, band, cols.shape[1]), bf16),
+            jax.ShapeDtypeStruct((lags - STEPS, *history.shape[1:]), bf16),
+        ),
         compiler_params=pltpu.CompilerParams(vmem_limit_bytes=48 << 20),
         name="old_mixed",
     )(history, cols)
 
 
-def field_kernel(first, fresh, incoming, cols, rows, mixed_old, out, newer):
-    band = incoming.shape[1]
+def field_kernel(first, core, fresh, mine, other, cols, rows, mixed_old, out, newer):
+    band = mine.shape[1]
     parts_in = fresh.shape[0] // STEPS
     ahead = []
     for n in range(STEPS):
-        density = [fresh[part * STEPS + STEPS - 1 - n] for part in range(parts_in)]
-        ahead.append(jnp.where(first[0] == 1, jnp.concatenate(density, axis=0), incoming[n]))
+        density = [fresh[(STEPS - 1 - n) * parts_in + part] for part in range(parts_in)]
+        older = jnp.where(core[0] == n // 2, mine[n % 2], other[n % 2])
+        ahead.append(jnp.where(first[0] == 1, jnp.concatenate(density, axis=0), older))
         newer[n] = ahead[n]
     grids = jnp.concatenate(ahead, axis=0)
     wide = cols.shape[1]
@@ -174,64 +201,62 @@
         field = lax.dot_general(lhs, rows[...], (((0,), (0,)), ((), ())), preferred_element_type=f32)
         field = field.astype(bf16)
         for band_to in range(bands):
-            out[band_to * STEPS + step] = field[band_to * share : (band_to + 1) * share]
-
-
-def field_parts(first, fresh, incoming, cols, rows, mixed_old, bands):
+            half, quarter = divmod(band_to, bands // 2)
+            out[(quarter * STEPS + step) * 2 + half] = field[band_to * share : (band_to + 1) * share]
+
+
+def field_parts(place, fresh, mine, other, cols, rows, mixed_old, bands):
     wide = cols.shape[1]
     vmem = pl.BlockSpec(memory_space=pltpu.VMEM)
     return pl.pallas_call(
         field_kernel,
-        in_specs=[pl.BlockSpec(memory_space=pltpu.SMEM)] + [vmem] * 5,
+        in_specs=[pl.BlockSpec(memory_space=pltpu.SMEM)] * 2 + [vmem] * 6,
         out_specs=(vmem, vmem),
         out_shape=(
             jax.ShapeDtypeStruct((bands * STEPS, wide // bands, rows.shape[1]), bf16),
-            jax.ShapeDtypeStruct(incoming.shape, bf16),
+            jax.ShapeDtypeStruct((STEPS, *mine.shape[1:]), bf16),
         ),
         compiler_params=pltpu.CompilerParams(vmem_limit_bytes=48 << 20),
         name="field_parts",
-    )(first, fresh, incoming, cols, rows, mixed_old)
+    )(*place, fresh, mine, other, cols, rows, mixed_old)
 
 
 def local(row_index, col_index, bin_index, charge, momentum, history, kernel_cols, kernel_rows):
     lags, band, _ = history.shape
     count = charge.shape[0]
     bands = NG // band
-    lines = count // LANES
     hist_at = lax.axis_index("hist")
     hist_size = lax.axis_size("hist")
 
-    fields = [row_index.astype(f32), col_index.astype(f32), bin_index.astype(f32)]
-    fields.append(jnp.broadcast_to(charge.astype(f32), (STEPS, count)))
-    packed = jnp.stack([x.reshape(STEPS, lines, LANES) for x in fields], axis=1)
-    packed = jnp.broadcast_to(packed.reshape(STEPS, 4 * lines, LANES), (2, STEPS, 4 * lines, LANES))
-    particles = swap(packed.reshape(2 * STEPS, 4 * lines, LANES), ("xh", "dom"))
+    particles = swap(pack(row_index, col_index, bin_index, charge, 2), ("dom", "xh"))
+    core = lax.axis_index("dom") % 2
     half = lax.axis_index("xh").reshape(1)
-
-    incoming = lax.ppermute(history[lags - STEPS :], "hist", [(i, i + 1) for i in range(hist_size - 1)])
-    mixed_old = old_mixed(history, kernel_cols)
+    place = [(hist_at == 0).astype(jnp.int32).reshape(1), core.reshape(1)]
+
+    mixed_old, kept = old_mixed(history, kernel_cols)
+    tail = lax.dynamic_slice_in_dim(history, lags - STEPS + 2 * core, 2, 0)
+    mine = lax.ppermute(tail, "hist", [(i, i + 1) for i in range(hist_size - 1)])
     rows_flat = kernel_rows.reshape(lags * band, 2 * NG)
 
     grid = deposit(half, particles, NG // 2, band, hist_size)
-    grid, incoming = lax.optimization_barrier((grid, incoming))
-    density = jnp.sum(swap(grid, ("hist", "y")).astype(f32), axis=0).astype(bf16)
-    fresh = to_all(density, ("hist", "dom"))
-
-    first = (hist_at == 0).astype(jnp.int32).reshape(1)
-    partial, ahead = field_parts(first, fresh, incoming, kernel_cols[:STEPS], rows_flat, mixed_old, bands)
-    received = swap(partial, ("xh", "y", "dom"))
+    grid, mine = lax.optimization_barrier((grid, mine))
+    other = lax.ppermute(mine, "dom", [(i, i ^ 1) for i in range(STEPS)])
+    density = jnp.sum(swap(grid, ("y", "hist")).astype(f32), axis=0).astype(bf16)
+    fresh = to_all(density, ("dom", "hist"))
+
+    partial, ahead = field_parts(place, fresh, mine, other, kernel_cols[:STEPS], rows_flat, mixed_old, bands)
+    received = swap(partial, ("y", "dom", "xh"))
     share = received.shape[1]
-    by_column = jnp.sum(received.reshape(bands, STEPS * share, 2 * NG).astype(f32), axis=0)
+    by_column = jnp.sum(received.reshape(bands // 2, STEPS, 2, share, 2 * NG).astype(f32), axis=(0, 2))
     by_column = by_column.reshape(hist_size, -1, 2 * NG)
     summed = jnp.sum(swap(by_column, "hist"), axis=0).astype(bf16)
-    whole = to_all(summed, "hist").reshape(STEPS * share, 2 * NG)
-    field = to_all(whole, "y").reshape(NG // 2, 2 * NG)
-
-    kick = swap(kicks(half, particles, field), ("xh", "dom"))
+    field = to_all(summed, ("y", "hist")).reshape(NG // 2, 2 * NG)
+
+    kick = swap(kicks(half, particles, field), ("dom", "xh"))
     kick_sum = jnp.sum(kick, axis=0).reshape(2, count)
     momentum_out = momentum + kick_scale * kick_sum
 
-    history_out = jnp.concatenate([ahead, history[: lags - STEPS]], axis=0)
+    history_out = jnp.concatenate([ahead, kept], axis=0)
     return momentum_out, history_out
 
 

time: 136 us -> 131 us (0.963)
  blocking collectives: 78.5 us -> 71 us
  starting transfers between devices: 21.7 us -> 27.7 us
  waiting for transfers between devices: 18.7 us -> 14.4 us
  Pallas kernels: 10.1 us -> 11.5 us
    all_to_all x5 -> x4, blocking collectives: 78.5 us -> 71 us  [swap(): return lax.all_to_all(array, axes, split_axis=0, concat_axis=0, tiled=True)]
    all_to_all x3, starting transfers between devices: 17.3 us -> 24.6 us  [swap(): return lax.all_to_all(array, axes, split_axis=0, concat_axis=0, tiled=True)]
    all_to_all x3, waiting for transfers between devices: 18.7 us -> 14.4 us  [swap(): return lax.all_to_all(array, axes, split_axis=0, concat_axis=0, tiled=True)]
    pallas_call x1 -> x2, Pallas kernels: 0.55 us -> 1.99 us  [the longest x1 1.45 us: pack(): pl.pallas_call(pack_kernel, in_specs=[vmem] * 4, out_specs=vmem, out_shap...]
    ppermute x1 -> x2, starting transfers between devices: 4.39 us -> 3.15 us  [the longest x1 2.83 us: local(): lax.ppermute(tail, 'hist', [(i, i + 1) for i in range(hist_size - 1)])]
  transfers between devices with their start and end apart: 4 -> 5, of which waited for: 3 -> 3; matrix products, arithmetic and copies ran while one was open for 2% -> 2% of each run, Pallas kernels for 2% -> 3%
where the time goes in v3:
time: 131 us; the launch traced here: 130 us
  blocking collectives  71 us (54%)
  starting transfers between devices  27.7 us (21%)
  waiting for transfers between devices  14.4 us (11%)
  Pallas kernels  11.5 us (9%)
  local copies, waits for them, and re-layouts  3.21 us (2%)
  other arithmetic  1.7 us (1%)
    all_to_all x4, blocking collectives, swap(): return lax.all_to_all(array, axes, split_axis=0, concat_axis=0, tiled=True)  71 us
    all_to_all x3, starting transfers between devices, swap(): return lax.all_to_all(array, axes, split_axis=0, concat_axis=0, tiled=True)  24.6 us
    all_to_all x3, waiting for transfers between devices, swap(): return lax.all_to_all(array, axes, split_axis=0, concat_axis=0, tiled=True)  14.4 us
    pallas_call x1, Pallas kernels, kicks(): pl.pallas_call(kick_kernel, in_specs=[pl.BlockSpec(memory_space=pltpu.SME...  5.65 us
    ppermute x1, starting transfers between devices, local(): lax.ppermute(tail, 'hist', [(i, i + 1) for i in range(hist_size - 1)])  2.83 us
    pallas_call x1, Pallas kernels, deposit(): pl.pallas_call(functools.partial(deposit_kernel, lines, band, parts), in_...  2.75 us
  transfers between devices with their start and end apart: 5, of which 3 were waited for; matrix products, arithmetic and copies ran while one was open for 2% of the time, Pallas kernels for 3%

profile of v3, /device:TPU:1, one launch (start us, length us, event | category | flops | bytes accessed | tf_op | source)
XLA Modules:
  0.0 130.2 jit_solution(8806470815703799893)
XLA Ops:
  0.6 1.4 %pack.1 = f32[8,4,1024]{2,1,0:T(4,128)} custom-call(s32[4,1024]{1,0:T(4,128)} %row.1, s32[4,1024]{1,0:T(4,128)} %col.1, s32[4,1024]{1,0:T(4,128)} %bins.1, bf16[1024]{0:T(1024)(128)(2,1)} %charge.1), custom_call_target="tpu_custom_call" | custom-call | tf_op jit(solution)/shard_map/pack/pallas_call | solution.py:67
  2.1 6.5 %all-to-all-start = ((f32[8,4,1024]{2,1,0:T(4,128)}), f32[8,4,1024]{2,1,0:T(4,128)S(1)}, u32[]{:S(2)}, u32[]{:S(2)}) async-start(f32[8,4,1024]{2,1,0:T(4,128)} %pack.1), calls=%async_computation | async-start | bytes 262144 | tf_op jit(solution)/shard_map/all_to_all | solution.py:21
  8.6 0.9 constant_dynamic-slice_fusion
  9.5 2.8 %collective-permute-start = (bf16[2,64,512]{2,1,0:T(8,128)(2,1)S(1)}, bf16[2,64,512]{2,1,0:T(8,128)(2,1)S(1)}, u32[]{:S(2)}, u32[]{:S(2)}) collective-permute-start(bf16[2,64,512]{2,1,0:T(8,128)(2,1)S(1)} %constant_dynamic-slice_fusion), channel_id=1, source_target_pairs={{0,32},{32,64},{64,96},{96,128},{128,160},{160,192},{192,224},{1,3... | collective-permute-start | bytes 393224 | tf_op jit(solution)/shard_map/ppermute | solution.py:238
  12.4 1.5 %all-to-all-done.particles = f32[8,4,1024]{2,1,0:T(4,128)S(1)} async-done(((f32[8,4,1024]{2,1,0:T(4,128)}), f32[8,4,1024]{2,1,0:T(4,128)S(1)}, u32[]{:S(2)}, u32[]{:S(2)}) %all-to-all-start) | async-done | bytes 131104 | tf_op jit(solution)/shard_map/all_to_all | solution.py:21
  13.9 2.8 %deposit.1 = bf16[32,8,512]{2,1,0:T(8,128)(2,1)S(1)} custom-call(s32[1]{0:T(128)} %bitcast.half, f32[8,4,1024]{2,1,0:T(4,128)S(1)} %all-to-all-done.particles), custom_call_target="tpu_custom_call" | custom-call | flops 4294967296 | bytes 1048576 | tf_op jit(solution)/shard_map/deposit/pallas_call | solution.py:98
  16.6 0.0 copy-start
  16.6 0.0 collective-permute-done.mine
  16.6 21.0 %all_to_all.35 = bf16[32,8,512]{2,1,0:T(8,128)(2,1)S(1)} all-to-all(bf16[32,8,512]{2,1,0:T(8,128)(2,1)S(1)} %deposit.1), channel_id=1, replica_groups=mesh['hist'=8,'xh'=2,'y'=4,'dom'=4] {'y','hist'}, dimensions={0} | all-to-all | bytes 524288 | tf_op jit(solution)/shard_map/all_to_all | solution.py:21
  37.7 0.0 copy-start.1
  37.7 0.1 reduce_sum.39
  37.7 0.7 broadcast_in_dim.6
  38.5 7.8 %all-to-all-start.2 = ((bf16[32,8,512]{2,1,0:T(8,128)(2,1)}), bf16[32,8,512]{2,1,0:T(8,128)(2,1)S(1)}, u32[]{:S(2)}, u32[]{:S(2)}) async-start(bf16[32,8,512]{2,1,0:T(8,128)(2,1)} %broadcast_in_dim.6), calls=%async_computation.2 | async-start | bytes 524288 | tf_op jit(solution)/shard_map/all_to_all | solution.py:21
  46.3 0.3 collective-permute-start.1
  46.6 0.0 copy-done
  46.7 0.0 copy-done.1
  46.7 0.5 old_mixed.1
  47.2 1.5 %copy.10 = bf16[64,8,2,512]{3,1,2,0:T(8,128)(2,1)S(1)} copy(bf16[64,8,2,512]{3,2,1,0:T(2,128)(2,1)} %bitcast.14) | data formatting | bytes 2097152
  48.7 0.0 collective-permute-done.1.other
  48.7 8.7 %all-to-all-done.2.fresh = bf16[32,8,512]{2,1,0:T(8,128)(2,1)S(1)} async-done(((bf16[32,8,512]{2,1,0:T(8,128)(2,1)}), bf16[32,8,512]{2,1,0:T(8,128)(2,1)S(1)}, u32[]{:S(2)}, u32[]{:S(2)}) %all-to-all-start.2) | async-done | bytes 262176 | tf_op jit(solution)/shard_map/all_to_all | solution.py:21
  57.5 1.1 field_parts.1
  58.5 21.6 %all_to_all.36 = bf16[32,16,1024]{2,1,0:T(8,128)(2,1)S(1)} all-to-all(bf16[32,16,1024]{2,1,0:T(8,128)(2,1)S(1)} %get-tuple-element.11), channel_id=1, replica_groups=mesh['hist'=8,'xh'=2,'y'=4,'dom'=4] {'y','dom','xh'}, dimensions={0} | all-to-all | bytes 2097152 | tf_op jit(solution)/shard_map/all_to_all | solution.py:21
  80.1 0.2 convert_reduce_fusion
  80.3 12.9 %all_to_all.37 = f32[8,8,1024]{2,1,0:T(8,128)S(1)} all-to-all(f32[8,8,1024]{2,1,0:T(8,128)S(1)} %bitcast.13), channel_id=1, replica_groups=mesh['hist'=8,'xh'=2,'y'=4,'dom'=4] {'hist'}, dimensions={0} | all-to-all | bytes 524288 | tf_op jit(solution)/shard_map/all_to_all | solution.py:21
  93.2 0.1 broadcast_in_dim.7
  93.3 15.5 %all_to_all.38 = bf16[32,8,1024]{2,1,0:T(8,128)(2,1)S(1)} all-to-all(bf16[32,8,1024]{2,1,0:T(8,128)(2,1)S(1)} %broadcast_in_dim.7), channel_id=1, replica_groups=mesh['hist'=8,'xh'=2,'y'=4,'dom'=4] {'y','hist'}, dimensions={0} | all-to-all | bytes 1048576 | tf_op jit(solution)/shard_map/all_to_all | solution.py:21
  108.8 0.0 copy-start.2
  108.8 5.6 %kicks.1 = f32[8,16,128]{2,1,0:T(8,128)} custom-call(s32[1]{0:T(128)} %bitcast.half, f32[8,4,1024]{2,1,0:T(4,128)S(1)} %all-to-all-done.particles, bf16[256,1024]{1,0:T(8,128)(2,1)S(1)} %bitcast.11), custom_call_target="tpu_custom_call" | custom-call | tf_op jit(solution)/shard_map/kicks/pallas_call | solution.py:139
  114.4 10.2 %all-to-all-start.6 = ((f32[8,16,128]{2,1,0:T(8,128)}), f32[8,16,128]{2,1,0:T(8,128)S(1)}, u32[]{:S(2)}, u32[]{:S(2)}) async-start(f32[8,16,128]{2,1,0:T(8,128)} %kicks.1), calls=%async_computation.6 | async-start | bytes 131072 | tf_op jit(solution)/shard_map/all_to_all | solution.py:21
  124.6 0.8 pad_maximum_fusion
  125.5 4.1 %all-to-all-done.6 = f32[8,16,128]{2,1,0:T(8,128)S(1)} async-done(((f32[8,16,128]{2,1,0:T(8,128)}), f32[8,16,128]{2,1,0:T(8,128)S(1)}, u32[]{:S(2)}, u32[]{:S(2)}) %all-to-all-start.6) | async-done | bytes 65568 | tf_op jit(solution)/shard_map/all_to_all | solution.py:21
  129.6 0.0 copy-done.2
  129.6 0.6 add.14
  (5 shorter events, 0.1 us)
Async XLA Ops:
  2.1 11.8 %all-to-all-start = ((f32[8,4,1024]{2,1,0:T(4,128)}), f32[8,4,1024]{2,1,0:T(4,128)S(1)}, u32[]{:S(2)}, u32[]{:S(2)}) async-start(f32[8,4,1024]{2,1,0:T(4,128)} %pack.1), calls=%async_computation | async-start | bytes 262144 | tf_op jit(solution)/shard_map/all_to_all | solution.py:21
  9.5 7.1 %collective-permute-start = (bf16[2,64,512]{2,1,0:T(8,128)(2,1)S(1)}, bf16[2,64,512]{2,1,0:T(8,128)(2,1)S(1)}, u32[]{:S(2)}, u32[]{:S(2)}) collective-permute-start(bf16[2,64,512]{2,1,0:T(8,128)(2,1)S(1)} %constant_dynamic-slice_fusion), channel_id=1, source_target_pairs={{0,32},{32,64},{64,96},{96,128},{128,160},{160,192},{192,224},{1,3... | collective-permute-start | bytes 393224 | tf_op jit(solution)/shard_map/ppermute | solution.py:238
  16.6 30.0 %copy-start = (bf16[8,128,512]{2,1,0:T(8,128)(2,1)S(1)}, bf16[8,128,512]{2,1,0:T(8,128)(2,1)}, u32[]{:S(2)}) copy-start(bf16[8,128,512]{2,1,0:T(8,128)(2,1)} %cols.1) | copy-start | bytes 3145732
  37.7 9.0 %copy-start.1 = (bf16[8,64,512]{2,1,0:T(8,128)(2,1)S(1)}, bf16[8,64,512]{2,1,0:T(8,128)(2,1)}, u32[]{:S(2)}) copy-start(bf16[8,64,512]{2,1,0:T(8,128)(2,1)} %history.1) | copy-start | bytes 1572868
  38.5 19.0 %all-to-all-start.2 = ((bf16[32,8,512]{2,1,0:T(8,128)(2,1)}), bf16[32,8,512]{2,1,0:T(8,128)(2,1)S(1)}, u32[]{:S(2)}, u32[]{:S(2)}) async-start(bf16[32,8,512]{2,1,0:T(8,128)(2,1)} %broadcast_in_dim.6), calls=%async_computation.2 | async-start | bytes 524288 | tf_op jit(solution)/shard_map/all_to_all | solution.py:21
  46.3 2.4 %collective-permute-start.1 = (bf16[2,64,512]{2,1,0:T(8,128)(2,1)S(1)}, bf16[2,64,512]{2,1,0:T(8,128)(2,1)S(1)}, u32[]{:S(2)}, u32[]{:S(2)}) collective-permute-start(bf16[2,64,512]{2,1,0:T(8,128)(2,1)S(1)} %collective-permute-done.mine), channel_id=1, source_target_pairs={{0,1},{1,0},{2,3},{3,2},{4,5},{5,4},{6,7},{7,6},{8,9},{9,8},{10,11... | collective-permute-start | bytes 393224 | tf_op jit(solution)/shard_map/ppermute | solution.py:243
  108.8 20.9 %copy-start.2 = (f32[2,1024]{1,0:T(2,128)S(1)}, f32[2,1024]{1,0:T(2,128)}, u32[]{:S(2)}) copy-start(f32[2,1024]{1,0:T(2,128)} %param.12) | copy-start | bytes 24580
  114.4 15.2 %all-to-all-start.6 = ((f32[8,16,128]{2,1,0:T(8,128)}), f32[8,16,128]{2,1,0:T(8,128)S(1)}, u32[]{:S(2)}, u32[]{:S(2)}) async-start(f32[8,16,128]{2,1,0:T(8,128)} %kicks.1), calls=%async_computation.6 | async-start | bytes 131072 | tf_op jit(solution)/shard_map/all_to_all | solution.py:21

commit v4 on v3

--- a/solution.py
+++ b/solution.py
@@ -158,7 +158,7 @@
     for step in range(STEPS):
         for lag in range(step + 1):
             out[step, lag] = jnp.zeros(out.shape[2:], bf16)
-    kept[...] = history[: lags - STEPS]
+    kept[STEPS:] = history[: lags - STEPS]
 
 
 def old_mixed(history, cols):
@@ -167,14 +167,14 @@
         old_mixed_kernel,
         out_shape=(
             jax.ShapeDtypeStruct((STEPS, lags, band, cols.shape[1]), bf16),
-            jax.ShapeDtypeStruct((lags - STEPS, *history.shape[1:]), bf16),
+            jax.ShapeDtypeStruct(history.shape, bf16),
         ),
         compiler_params=pltpu.CompilerParams(vmem_limit_bytes=48 << 20),
         name="old_mixed",
     )(history, cols)
 
 
-def field_kernel(first, core, fresh, mine, other, cols, rows, mixed_old, out, newer):
+def field_kernel(first, core, fresh, mine, other, cols, rows, mixed_old, kept, out, cycle, newer, sem):
     band = mine.shape[1]
     parts_in = fresh.shape[0] // STEPS
     ahead = []
@@ -183,6 +183,8 @@
         older = jnp.where(core[0] == n // 2, mine[n % 2], other[n % 2])
         ahead.append(jnp.where(first[0] == 1, jnp.concatenate(density, axis=0), older))
         newer[n] = ahead[n]
+    store = pltpu.make_async_copy(newer, cycle.at[pl.ds(0, STEPS)], sem)
+    store.start()
     grids = jnp.concatenate(ahead, axis=0)
     wide = cols.shape[1]
     parts = [[] for _ in range(STEPS)]
@@ -203,22 +205,25 @@
         for band_to in range(bands):
             half, quarter = divmod(band_to, bands // 2)
             out[(quarter * STEPS + step) * 2 + half] = field[band_to * share : (band_to + 1) * share]
-
-
-def field_parts(place, fresh, mine, other, cols, rows, mixed_old, bands):
+    store.wait()
+
+
+def field_parts(place, fresh, mine, other, cols, rows, mixed_old, kept, bands):
     wide = cols.shape[1]
     vmem = pl.BlockSpec(memory_space=pltpu.VMEM)
     return pl.pallas_call(
         field_kernel,
-        in_specs=[pl.BlockSpec(memory_space=pltpu.SMEM)] * 2 + [vmem] * 6,
-        out_specs=(vmem, vmem),
+        in_specs=[pl.BlockSpec(memory_space=pltpu.SMEM)] * 2 + [vmem] * 6 + [pl.BlockSpec(memory_space=pl.ANY)],
+        out_specs=(vmem, pl.BlockSpec(memory_space=pl.ANY)),
         out_shape=(
             jax.ShapeDtypeStruct((bands * STEPS, wide // bands, rows.shape[1]), bf16),
-            jax.ShapeDtypeStruct((STEPS, *mine.shape[1:]), bf16),
+            jax.ShapeDtypeStruct(kept.shape, bf16),
         ),
+        scratch_shapes=[pltpu.VMEM((STEPS, *mine.shape[1:]), bf16), pltpu.SemaphoreType.DMA],
+        input_output_aliases={8: 1},
         compiler_params=pltpu.CompilerParams(vmem_limit_bytes=48 << 20),
         name="field_parts",
-    )(*place, fresh, mine, other, cols, rows, mixed_old)
+    )(*place, fresh, mine, other, cols, rows, mixed_old, kept)
 
 
 def local(row_index, col_index, bin_index, charge, momentum, history, kernel_cols, kernel_rows):
@@ -244,7 +249,9 @@
     density = jnp.sum(swap(grid, ("y", "hist")).astype(f32), axis=0).astype(bf16)
     fresh = to_all(density, ("dom", "hist"))
 
-    partial, ahead = field_parts(place, fresh, mine, other, kernel_cols[:STEPS], rows_flat, mixed_old, bands)
+    partial, history_out = field_parts(
+        place, fresh, mine, other, kernel_cols[:STEPS], rows_flat, mixed_old, kept, bands
+    )
     received = swap(partial, ("y", "dom", "xh"))
     share = received.shape[1]
     by_column = jnp.sum(received.reshape(bands // 2, STEPS, 2, share, 2 * NG).astype(f32), axis=(0, 2))
@@ -256,7 +263,6 @@
     kick_sum = jnp.sum(kick, axis=0).reshape(2, count)
     momentum_out = momentum + kick_scale * kick_sum
 
-    history_out = jnp.concatenate([ahead, kept], axis=0)
     return momentum_out, history_out
 
 

time: 131 us -> 130 us (level)
  blocking collectives: 71 us -> 86 us
  starting transfers between devices: 27.7 us -> 17.5 us
  waiting for transfers between devices: 14.4 us -> 9.54 us
    all_to_all x4 -> x5, blocking collectives: 71 us -> 86 us  [swap(): return lax.all_to_all(array, axes, split_axis=0, concat_axis=0, tiled=True)]
    all_to_all x3 -> x2, starting transfers between devices: 24.6 us -> 14.4 us  [swap(): return lax.all_to_all(array, axes, split_axis=0, concat_axis=0, tiled=True)]
    all_to_all x3 -> x2, waiting for transfers between devices: 14.4 us -> 9.54 us  [swap(): return lax.all_to_all(array, axes, split_axis=0, concat_axis=0, tiled=True)]
  transfers between devices with their start and end apart: 5 -> 4, of which waited for: 3 -> 2; matrix products, arithmetic and copies ran while one was open for 2% -> 2% of each run, Pallas kernels for 3% -> 3%
where the time goes in v4:
time: 130 us; the launch traced here: 129 us
  blocking collectives  86 us (66%)
  starting transfers between devices  17.5 us (13%)
  Pallas kernels  11.5 us (9%)
  waiting for transfers between devices  9.54 us (7%)
  local copies, waits for them, and re-layouts  3.2 us (2%)
    all_to_all x5, blocking collectives, swap(): return lax.all_to_all(array, axes, split_axis=0, concat_axis=0, tiled=True)  86 us
    all_to_all x2, starting transfers between devices, swap(): return lax.all_to_all(array, axes, split_axis=0, concat_axis=0, tiled=True)  14.4 us
    all_to_all x2, waiting for transfers between devices, swap(): return lax.all_to_all(array, axes, split_axis=0, concat_axis=0, tiled=True)  9.54 us
    pallas_call x1, Pallas kernels, kicks(): pl.pallas_call(kick_kernel, in_specs=[pl.BlockSpec(memory_space=pltpu.SME...  4.93 us
    ppermute x1, starting transfers between devices, local(): lax.ppermute(tail, 'hist', [(i, i + 1) for i in range(hist_size - 1)])  2.83 us
    pallas_call x1, Pallas kernels, deposit(): pl.pallas_call(functools.partial(deposit_kernel, lines, band, parts), in_...  2.75 us
  transfers between devices with their start and end apart: 4, of which 2 were waited for; matrix products, arithmetic and copies ran while one was open for 2% of the time, Pallas kernels for 3%

profile of v4, /device:TPU:1, one launch (start us, length us, event | category | flops | bytes accessed | tf_op | source)
XLA Modules:
  0.0 129.3 jit_solution(12983581031332028318)
XLA Ops:
  0.6 1.4 %pack.1 = f32[8,4,1024]{2,1,0:T(4,128)} custom-call(s32[4,1024]{1,0:T(4,128)} %row.1, s32[4,1024]{1,0:T(4,128)} %col.1, s32[4,1024]{1,0:T(4,128)} %bins.1, bf16[1024]{0:T(1024)(128)(2,1)} %charge.1), custom_call_target="tpu_custom_call" | custom-call | tf_op jit(solution)/shard_map/pack/pallas_call | solution.py:67
  2.1 6.5 %all-to-all-start = ((f32[8,4,1024]{2,1,0:T(4,128)}), f32[8,4,1024]{2,1,0:T(4,128)S(1)}, u32[]{:S(2)}, u32[]{:S(2)}) async-start(f32[8,4,1024]{2,1,0:T(4,128)} %pack.1), calls=%async_computation | async-start | bytes 262144 | tf_op jit(solution)/shard_map/all_to_all | solution.py:21
  8.6 0.9 constant_dynamic-slice_fusion
  9.5 2.8 %collective-permute-start = (bf16[2,64,512]{2,1,0:T(8,128)(2,1)S(1)}, bf16[2,64,512]{2,1,0:T(8,128)(2,1)S(1)}, u32[]{:S(2)}, u32[]{:S(2)}) collective-permute-start(bf16[2,64,512]{2,1,0:T(8,128)(2,1)S(1)} %constant_dynamic-slice_fusion), channel_id=1, source_target_pairs={{0,32},{32,64},{64,96},{96,128},{128,160},{160,192},{192,224},{1,3... | collective-permute-start | bytes 393224 | tf_op jit(solution)/shard_map/ppermute | solution.py:243
  12.4 1.5 %all-to-all-done.particles = f32[8,4,1024]{2,1,0:T(4,128)S(1)} async-done(((f32[8,4,1024]{2,1,0:T(4,128)}), f32[8,4,1024]{2,1,0:T(4,128)S(1)}, u32[]{:S(2)}, u32[]{:S(2)}) %all-to-all-start) | async-done | bytes 131104 | tf_op jit(solution)/shard_map/all_to_all | solution.py:21
  13.9 2.8 %deposit.1 = bf16[32,8,512]{2,1,0:T(8,128)(2,1)S(1)} custom-call(s32[1]{0:T(128)} %bitcast.half, f32[8,4,1024]{2,1,0:T(4,128)S(1)} %all-to-all-done.particles), custom_call_target="tpu_custom_call" | custom-call | flops 4294967296 | bytes 1048576 | tf_op jit(solution)/shard_map/deposit/pallas_call | solution.py:98
  16.6 0.0 copy-start
  16.6 0.0 collective-permute-done.mine
  16.6 21.0 %all_to_all.35 = bf16[32,8,512]{2,1,0:T(8,128)(2,1)S(1)} all-to-all(bf16[32,8,512]{2,1,0:T(8,128)(2,1)S(1)} %deposit.1), channel_id=1, replica_groups=mesh['hist'=8,'xh'=2,'y'=4,'dom'=4] {'y','hist'}, dimensions={0} | all-to-all | bytes 524288 | tf_op jit(solution)/shard_map/all_to_all | solution.py:21
  37.7 0.0 copy-start.1
  37.7 0.1 reduce_sum.39
  37.7 0.7 broadcast_in_dim.6
  38.5 7.8 %all-to-all-start.2 = ((bf16[32,8,512]{2,1,0:T(8,128)(2,1)}), bf16[32,8,512]{2,1,0:T(8,128)(2,1)S(1)}, u32[]{:S(2)}, u32[]{:S(2)}) async-start(bf16[32,8,512]{2,1,0:T(8,128)(2,1)} %broadcast_in_dim.6), calls=%async_computation.2 | async-start | bytes 524288 | tf_op jit(solution)/shard_map/all_to_all | solution.py:21
  46.3 0.3 collective-permute-start.1
  46.6 0.0 copy-done
  46.7 0.0 copy-done.1
  46.7 1.3 old_mixed.1
  48.0 1.5 %copy.11 = bf16[64,8,2,512]{3,1,2,0:T(8,128)(2,1)S(1)} copy(bf16[64,8,2,512]{3,2,1,0:T(2,128)(2,1)} %bitcast.14) | data formatting | bytes 2097152
  49.4 0.0 collective-permute-done.1.other
  49.4 8.0 %all-to-all-done.2.fresh = bf16[32,8,512]{2,1,0:T(8,128)(2,1)S(1)} async-done(((bf16[32,8,512]{2,1,0:T(8,128)(2,1)}), bf16[32,8,512]{2,1,0:T(8,128)(2,1)S(1)}, u32[]{:S(2)}, u32[]{:S(2)}) %all-to-all-start.2) | async-done | bytes 262176 | tf_op jit(solution)/shard_map/all_to_all | solution.py:21
  57.5 1.1 field_parts.1
  58.6 21.6 %all_to_all.36 = bf16[32,16,1024]{2,1,0:T(8,128)(2,1)S(1)} all-to-all(bf16[32,16,1024]{2,1,0:T(8,128)(2,1)S(1)} %get-tuple-element.12), channel_id=1, replica_groups=mesh['hist'=8,'xh'=2,'y'=4,'dom'=4] {'y','dom','xh'}, dimensions={0} | all-to-all | bytes 2097152 | tf_op jit(solution)/shard_map/all_to_all | solution.py:21
  80.2 0.2 convert_reduce_fusion
  80.3 12.9 %all_to_all.37 = f32[8,8,1024]{2,1,0:T(8,128)S(1)} all-to-all(f32[8,8,1024]{2,1,0:T(8,128)S(1)} %bitcast.13), channel_id=1, replica_groups=mesh['hist'=8,'xh'=2,'y'=4,'dom'=4] {'hist'}, dimensions={0} | all-to-all | bytes 524288 | tf_op jit(solution)/shard_map/all_to_all | solution.py:21
  93.2 0.1 broadcast_in_dim.7
  93.3 0.0 copy-start.2
  93.3 15.5 %all_to_all.38 = bf16[32,8,1024]{2,1,0:T(8,128)(2,1)S(1)} all-to-all(bf16[32,8,1024]{2,1,0:T(8,128)(2,1)S(1)} %broadcast_in_dim.7), channel_id=1, replica_groups=mesh['hist'=8,'xh'=2,'y'=4,'dom'=4] {'y','hist'}, dimensions={0} | all-to-all | bytes 1048576 | tf_op jit(solution)/shard_map/all_to_all | solution.py:21
  108.8 4.9 %kicks.1 = f32[8,16,128]{2,1,0:T(8,128)S(1)} custom-call(s32[1]{0:T(128)} %bitcast.half, f32[8,4,1024]{2,1,0:T(4,128)S(1)} %all-to-all-done.particles, bf16[256,1024]{1,0:T(8,128)(2,1)S(1)} %bitcast.11), custom_call_target="tpu_custom_call" | custom-call | tf_op jit(solution)/shard_map/kicks/pallas_call | solution.py:139
  113.7 15.0 %all_to_all.39 = f32[8,16,128]{2,1,0:T(8,128)S(1)} all-to-all(f32[8,16,128]{2,1,0:T(8,128)S(1)} %kicks.1), channel_id=1, replica_groups=mesh['hist'=8,'xh'=2,'y'=4,'dom'=4] {'dom','xh'}, dimensions={0} | all-to-all | bytes 131072 | tf_op jit(solution)/shard_map/all_to_all | solution.py:21
  128.7 0.0 copy-done.2
  128.7 0.6 add.14
  (5 shorter events, 0.1 us)
Async XLA Ops:
  2.1 11.8 %all-to-all-start = ((f32[8,4,1024]{2,1,0:T(4,128)}), f32[8,4,1024]{2,1,0:T(4,128)S(1)}, u32[]{:S(2)}, u32[]{:S(2)}) async-start(f32[8,4,1024]{2,1,0:T(4,128)} %pack.1), calls=%async_computation | async-start | bytes 262144 | tf_op jit(solution)/shard_map/all_to_all | solution.py:21
  9.5 7.1 %collective-permute-start = (bf16[2,64,512]{2,1,0:T(8,128)(2,1)S(1)}, bf16[2,64,512]{2,1,0:T(8,128)(2,1)S(1)}, u32[]{:S(2)}, u32[]{:S(2)}) collective-permute-start(bf16[2,64,512]{2,1,0:T(8,128)(2,1)S(1)} %constant_dynamic-slice_fusion), channel_id=1, source_target_pairs={{0,32},{32,64},{64,96},{96,128},{128,160},{160,192},{192,224},{1,3... | collective-permute-start | bytes 393224 | tf_op jit(solution)/shard_map/ppermute | solution.py:243
  16.6 30.0 %copy-start = (bf16[8,128,512]{2,1,0:T(8,128)(2,1)S(1)}, bf16[8,128,512]{2,1,0:T(8,128)(2,1)}, u32[]{:S(2)}) copy-start(bf16[8,128,512]{2,1,0:T(8,128)(2,1)} %cols.1) | copy-start | bytes 3145732
  37.7 9.0 %copy-start.1 = (bf16[8,64,512]{2,1,0:T(8,128)(2,1)S(1)}, bf16[8,64,512]{2,1,0:T(8,128)(2,1)}, u32[]{:S(2)}) copy-start(bf16[8,64,512]{2,1,0:T(8,128)(2,1)} %history.1) | copy-start | bytes 1572868
  38.5 19.0 %all-to-all-start.2 = ((bf16[32,8,512]{2,1,0:T(8,128)(2,1)}), bf16[32,8,512]{2,1,0:T(8,128)(2,1)S(1)}, u32[]{:S(2)}, u32[]{:S(2)}) async-start(bf16[32,8,512]{2,1,0:T(8,128)(2,1)} %broadcast_in_dim.6), calls=%async_computation.2 | async-start | bytes 524288 | tf_op jit(solution)/shard_map/all_to_all | solution.py:21
  46.3 3.1 %collective-permute-start.1 = (bf16[2,64,512]{2,1,0:T(8,128)(2,1)S(1)}, bf16[2,64,512]{2,1,0:T(8,128)(2,1)S(1)}, u32[]{:S(2)}, u32[]{:S(2)}) collective-permute-start(bf16[2,64,512]{2,1,0:T(8,128)(2,1)S(1)} %collective-permute-done.mine), channel_id=1, source_target_pairs={{0,1},{1,0},{2,3},{3,2},{4,5},{5,4},{6,7},{7,6},{8,9},{9,8},{10,11... | collective-permute-start | bytes 393224 | tf_op jit(solution)/shard_map/ppermute | solution.py:248
  93.3 35.5 %copy-start.2 = (f32[2,1024]{1,0:T(2,128)S(1)}, f32[2,1024]{1,0:T(2,128)}, u32[]{:S(2)}) copy-start(f32[2,1024]{1,0:T(2,128)} %param.12) | copy-start | bytes 24580

commit v5 on v4

--- a/solution.py
+++ b/solution.py
@@ -50,7 +50,11 @@
     return lax.broadcasted_iota(jnp.int32, (count, size), 0)
 
 
-def pack_kernel(row, col, bins, charge, out):
+def pack_kernel(core, row, col, bins, charge, history, out, tail, sem):
+    count_out = tail.shape[0]
+    first = history.shape[0] - STEPS + count_out * core[0]
+    fetch = pltpu.make_async_copy(history.at[pl.ds(first, count_out)], tail, sem)
+    fetch.start()
     steps, count = row.shape
     weight = charge[...].astype(f32).reshape(1, count)
     halves = out.shape[0] // steps
@@ -59,18 +63,23 @@
         packed = jnp.concatenate(fields + [weight], axis=0)
         for half in range(halves):
             out[step * halves + half] = packed
-
-
-def pack(row, col, bins, charge, halves):
+    fetch.wait()
+
+
+def pack(core, row, col, bins, charge, history, halves):
     steps, count = row.shape
     vmem = pl.BlockSpec(memory_space=pltpu.VMEM)
     return pl.pallas_call(
         pack_kernel,
-        in_specs=[vmem] * 4,
-        out_specs=vmem,
-        out_shape=jax.ShapeDtypeStruct((halves * steps, 4, count), f32),
+        in_specs=[pl.BlockSpec(memory_space=pltpu.SMEM)] + [vmem] * 4 + [pl.BlockSpec(memory_space=pl.ANY)],
+        out_specs=(vmem, pl.BlockSpec(memory_space=pl.ANY)),
+        out_shape=(
+            jax.ShapeDtypeStruct((halves * steps, 4, count), f32),
+            jax.ShapeDtypeStruct((2, *history.shape[1:]), bf16),
+        ),
+        scratch_shapes=[pltpu.SemaphoreType.DMA],
         name="pack",
-    )(row, col, bins, charge)
+    )(core, row, col, bins, charge, history)
 
 
 def deposit_kernel(lines, band, parts, half, particles, out):
@@ -233,13 +242,13 @@
     hist_at = lax.axis_index("hist")
     hist_size = lax.axis_size("hist")
 
-    particles = swap(pack(row_index, col_index, bin_index, charge, 2), ("dom", "xh"))
     core = lax.axis_index("dom") % 2
+    packed, tail = pack(core.reshape(1), row_index, col_index, bin_index, charge, history, 2)
+    particles = swap(packed, ("dom", "xh"))
     half = lax.axis_index("xh").reshape(1)
     place = [(hist_at == 0).astype(jnp.int32).reshape(1), core.reshape(1)]
 
     mixed_old, kept = old_mixed(history, kernel_cols)
-    tail = lax.dynamic_slice_in_dim(history, lags - STEPS + 2 * core, 2, 0)
     mine = lax.ppermute(tail, "hist", [(i, i + 1) for i in range(hist_size - 1)])
     rows_flat = kernel_rows.reshape(lags * band, 2 * NG)
 

time: 130 us -> 134 us (1.031)
  Pallas kernels: 11.5 us -> 16.5 us
    pallas_call x1, Pallas kernels: 1.45 us -> 6.49 us  [pack(): pl.pallas_call(pack_kernel, in_specs=[pl.BlockSpec(memory_space=pltpu.SME...]
  transfers between devices with their start and end apart: 4 -> 4, of which waited for: 2 -> 2; matrix products, arithmetic and copies ran while one was open for 2% -> 1% of each run, Pallas kernels for 3% -> 3%
where the time goes in v5:
time: 134 us
  blocking collectives  85.2 us (64%)
  starting transfers between devices  17.5 us (13%)
  Pallas kernels  16.5 us (12%)
  waiting for transfers between devices  10.5 us (8%)
  local copies, waits for them, and re-layouts  2.29 us (2%)
    all_to_all x5, blocking collectives, swap(): return lax.all_to_all(array, axes, split_axis=0, concat_axis=0, tiled=True)  85.2 us
    all_to_all x2, starting transfers between devices, swap(): return lax.all_to_all(array, axes, split_axis=0, concat_axis=0, tiled=True)  14.4 us
    all_to_all x2, waiting for transfers between devices, swap(): return lax.all_to_all(array, axes, split_axis=0, concat_axis=0, tiled=True)  10.5 us
    pallas_call x1, Pallas kernels, pack(): pl.pallas_call(pack_kernel, in_specs=[pl.BlockSpec(memory_space=pltpu.SME...  6.49 us
    pallas_call x1, Pallas kernels, kicks(): pl.pallas_call(kick_kernel, in_specs=[pl.BlockSpec(memory_space=pltpu.SME...  4.93 us
    ppermute x1, starting transfers between devices, local(): lax.ppermute(tail, 'hist', [(i, i + 1) for i in range(hist_size - 1)])  2.82 us
    pallas_call x1, Pallas kernels, deposit(): pl.pallas_call(functools.partial(deposit_kernel, lines, band, parts), in_...  2.75 us
  transfers between devices with their start and end apart: 4, of which 2 were waited for; matrix products, arithmetic and copies ran while one was open for 1% of the time, Pallas kernels for 3%

profile of v5, /device:TPU:1, one launch (start us, length us, event | category | flops | bytes accessed | tf_op | source)
XLA Modules:
  0.0 133.7 jit_solution(15165242908123942054)
XLA Ops:
  0.6 6.5 %pack.1 = (f32[8,4,1024]{2,1,0:T(4,128)}, bf16[2,64,512]{2,1,0:T(8,128)(2,1)}) custom-call(s32[1]{0:T(128)} %bitcast.1.core, s32[4,1024]{1,0:T(4,128)} %row.1, s32[4,1024]{1,0:T(4,128)} %col.1, s32[4,1024]{1,0:T(4,128)} %bins.1, bf16[1024]{0:T(1024)(128)(2,1)} %charge.1, bf16[8,64,512]{2,1,0:T(8,128)(2,1)} %history.3), custom_call_target="tpu_custom_call" | custom-call | tf_op jit(solution)/shard_map/pack/pallas_call | solution.py:72
  7.1 6.5 %all-to-all-start = ((f32[8,4,1024]{2,1,0:T(4,128)}), f32[8,4,1024]{2,1,0:T(4,128)S(1)}, u32[]{:S(2)}, u32[]{:S(2)}) async-start(f32[8,4,1024]{2,1,0:T(4,128)} %get-tuple-element.10), calls=%async_computation | async-start | bytes 262144 | tf_op jit(solution)/shard_map/all_to_all | solution.py:21
  13.7 2.8 %collective-permute-start = (bf16[2,64,512]{2,1,0:T(8,128)(2,1)}, bf16[2,64,512]{2,1,0:T(8,128)(2,1)S(1)}, u32[]{:S(2)}, u32[]{:S(2)}) collective-permute-start(bf16[2,64,512]{2,1,0:T(8,128)(2,1)} %get-tuple-element.11), channel_id=1, source_target_pairs={{0,32},{32,64},{64,96},{96,128},{128,160},{160,192},{192,224},{1,3... | collective-permute-start | bytes 393224 | tf_op jit(solution)/shard_map/ppermute | solution.py:252
  16.5 2.4 %all-to-all-done.particles = f32[8,4,1024]{2,1,0:T(4,128)S(1)} async-done(((f32[8,4,1024]{2,1,0:T(4,128)}), f32[8,4,1024]{2,1,0:T(4,128)S(1)}, u32[]{:S(2)}, u32[]{:S(2)}) %all-to-all-start) | async-done | bytes 131104 | tf_op jit(solution)/shard_map/all_to_all | solution.py:21
  18.9 2.8 %deposit.1 = bf16[32,8,512]{2,1,0:T(8,128)(2,1)S(1)} custom-call(s32[1]{0:T(128)} %bitcast.half, f32[8,4,1024]{2,1,0:T(4,128)S(1)} %all-to-all-done.particles), custom_call_target="tpu_custom_call" | custom-call | flops 4294967296 | bytes 1048576 | tf_op jit(solution)/shard_map/deposit/pallas_call | solution.py:107
  21.7 0.0 copy-start
  21.7 0.0 collective-permute-done.mine
  21.7 20.3 %all_to_all.35 = bf16[32,8,512]{2,1,0:T(8,128)(2,1)S(1)} all-to-all(bf16[32,8,512]{2,1,0:T(8,128)(2,1)S(1)} %deposit.1), channel_id=1, replica_groups=mesh['hist'=8,'xh'=2,'y'=4,'dom'=4] {'y','hist'}, dimensions={0} | all-to-all | bytes 524288 | tf_op jit(solution)/shard_map/all_to_all | solution.py:21
  42.0 0.0 copy-start.1
  42.0 0.1 reduce_sum.39
  42.1 0.7 broadcast_in_dim.6
  42.8 7.8 %all-to-all-start.2 = ((bf16[32,8,512]{2,1,0:T(8,128)(2,1)}), bf16[32,8,512]{2,1,0:T(8,128)(2,1)S(1)}, u32[]{:S(2)}, u32[]{:S(2)}) async-start(bf16[32,8,512]{2,1,0:T(8,128)(2,1)} %broadcast_in_dim.6), calls=%async_computation.2 | async-start | bytes 524288 | tf_op jit(solution)/shard_map/all_to_all | solution.py:21
  50.7 0.3 collective-permute-start.1
  51.0 0.0 copy-done
  51.0 0.0 copy-done.1
  51.0 1.3 old_mixed.1
  52.3 1.5 %copy.11 = bf16[64,8,2,512]{3,1,2,0:T(8,128)(2,1)S(1)} copy(bf16[64,8,2,512]{3,2,1,0:T(2,128)(2,1)} %bitcast.14) | data formatting | bytes 2097152
  53.8 0.0 collective-permute-done.1.other
  53.8 8.0 %all-to-all-done.2.fresh = bf16[32,8,512]{2,1,0:T(8,128)(2,1)S(1)} async-done(((bf16[32,8,512]{2,1,0:T(8,128)(2,1)}), bf16[32,8,512]{2,1,0:T(8,128)(2,1)S(1)}, u32[]{:S(2)}, u32[]{:S(2)}) %all-to-all-start.2) | async-done | bytes 262176 | tf_op jit(solution)/shard_map/all_to_all | solution.py:21
  61.8 1.1 field_parts.1
  62.9 21.6 %all_to_all.36 = bf16[32,16,1024]{2,1,0:T(8,128)(2,1)S(1)} all-to-all(bf16[32,16,1024]{2,1,0:T(8,128)(2,1)S(1)} %get-tuple-element.16), channel_id=1, replica_groups=mesh['hist'=8,'xh'=2,'y'=4,'dom'=4] {'y','dom','xh'}, dimensions={0} | all-to-all | bytes 2097152 | tf_op jit(solution)/shard_map/all_to_all | solution.py:21
  84.5 0.2 convert_reduce_fusion
  84.7 12.9 %all_to_all.37 = f32[8,8,1024]{2,1,0:T(8,128)S(1)} all-to-all(f32[8,8,1024]{2,1,0:T(8,128)S(1)} %bitcast.13), channel_id=1, replica_groups=mesh['hist'=8,'xh'=2,'y'=4,'dom'=4] {'hist'}, dimensions={0} | all-to-all | bytes 524288 | tf_op jit(solution)/shard_map/all_to_all | solution.py:21
  97.6 0.1 broadcast_in_dim.7
  97.6 0.0 copy-start.2
  97.6 15.5 %all_to_all.38 = bf16[32,8,1024]{2,1,0:T(8,128)(2,1)S(1)} all-to-all(bf16[32,8,1024]{2,1,0:T(8,128)(2,1)S(1)} %broadcast_in_dim.7), channel_id=1, replica_groups=mesh['hist'=8,'xh'=2,'y'=4,'dom'=4] {'y','hist'}, dimensions={0} | all-to-all | bytes 1048576 | tf_op jit(solution)/shard_map/all_to_all | solution.py:21
  113.1 4.9 %kicks.1 = f32[8,16,128]{2,1,0:T(8,128)S(1)} custom-call(s32[1]{0:T(128)} %bitcast.half, f32[8,4,1024]{2,1,0:T(4,128)S(1)} %all-to-all-done.particles, bf16[256,1024]{1,0:T(8,128)(2,1)S(1)} %bitcast.11), custom_call_target="tpu_custom_call" | custom-call | tf_op jit(solution)/shard_map/kicks/pallas_call | solution.py:148
  118.1 15.0 %all_to_all.39 = f32[8,16,128]{2,1,0:T(8,128)S(1)} all-to-all(f32[8,16,128]{2,1,0:T(8,128)S(1)} %kicks.1), channel_id=1, replica_groups=mesh['hist'=8,'xh'=2,'y'=4,'dom'=4] {'dom','xh'}, dimensions={0} | all-to-all | bytes 131072 | tf_op jit(solution)/shard_map/all_to_all | solution.py:21
  133.1 0.0 copy-done.2
  133.1 0.6 add.8
  (5 shorter events, 0.1 us)
Async XLA Ops:
  7.1 11.8 %all-to-all-start = ((f32[8,4,1024]{2,1,0:T(4,128)}), f32[8,4,1024]{2,1,0:T(4,128)S(1)}, u32[]{:S(2)}, u32[]{:S(2)}) async-start(f32[8,4,1024]{2,1,0:T(4,128)} %get-tuple-element.10), calls=%async_computation | async-start | bytes 262144 | tf_op jit(solution)/shard_map/all_to_all | solution.py:21
  13.7 8.0 %collective-permute-start = (bf16[2,64,512]{2,1,0:T(8,128)(2,1)}, bf16[2,64,512]{2,1,0:T(8,128)(2,1)S(1)}, u32[]{:S(2)}, u32[]{:S(2)}) collective-permute-start(bf16[2,64,512]{2,1,0:T(8,128)(2,1)} %get-tuple-element.11), channel_id=1, source_target_pairs={{0,32},{32,64},{64,96},{96,128},{128,160},{160,192},{192,224},{1,3... | collective-permute-start | bytes 393224 | tf_op jit(solution)/shard_map/ppermute | solution.py:252
  21.7 29.3 %copy-start = (bf16[8,128,512]{2,1,0:T(8,128)(2,1)S(1)}, bf16[8,128,512]{2,1,0:T(8,128)(2,1)}, u32[]{:S(2)}) copy-start(bf16[8,128,512]{2,1,0:T(8,128)(2,1)} %cols.1) | copy-start | bytes 3145732
  42.0 9.0 %copy-start.1 = (bf16[8,64,512]{2,1,0:T(8,128)(2,1)S(1)}, bf16[8,64,512]{2,1,0:T(8,128)(2,1)}, u32[]{:S(2)}) copy-start(bf16[8,64,512]{2,1,0:T(8,128)(2,1)} %history.3) | copy-start | bytes 1572868
  42.8 19.0 %all-to-all-start.2 = ((bf16[32,8,512]{2,1,0:T(8,128)(2,1)}), bf16[32,8,512]{2,1,0:T(8,128)(2,1)S(1)}, u32[]{:S(2)}, u32[]{:S(2)}) async-start(bf16[32,8,512]{2,1,0:T(8,128)(2,1)} %broadcast_in_dim.6), calls=%async_computation.2 | async-start | bytes 524288 | tf_op jit(solution)/shard_map/all_to_all | solution.py:21
  50.7 3.1 %collective-permute-start.1 = (bf16[2,64,512]{2,1,0:T(8,128)(2,1)S(1)}, bf16[2,64,512]{2,1,0:T(8,128)(2,1)S(1)}, u32[]{:S(2)}, u32[]{:S(2)}) collective-permute-start(bf16[2,64,512]{2,1,0:T(8,128)(2,1)S(1)} %collective-permute-done.mine), channel_id=1, source_target_pairs={{0,1},{1,0},{2,3},{3,2},{4,5},{5,4},{6,7},{7,6},{8,9},{9,8},{10,11... | collective-permute-start | bytes 393224 | tf_op jit(solution)/shard_map/ppermute | solution.py:257
  97.6 35.5 %copy-start.2 = (f32[2,1024]{1,0:T(2,128)S(1)}, f32[2,1024]{1,0:T(2,128)}, u32[]{:S(2)}) copy-start(f32[2,1024]{1,0:T(2,128)} %param.12) | copy-start | bytes 24580

commit v6 on v5

--- a/solution.py
+++ b/solution.py
@@ -72,7 +72,7 @@
     return pl.pallas_call(
         pack_kernel,
         in_specs=[pl.BlockSpec(memory_space=pltpu.SMEM)] + [vmem] * 4 + [pl.BlockSpec(memory_space=pl.ANY)],
-        out_specs=(vmem, pl.BlockSpec(memory_space=pl.ANY)),
+        out_specs=(vmem, vmem),
         out_shape=(
             jax.ShapeDtypeStruct((halves * steps, 4, count), f32),
             jax.ShapeDtypeStruct((2, *history.shape[1:]), bf16),

time: 134 us -> 130 us (0.970)
  Pallas kernels: 16.5 us -> 12.4 us
    pallas_call x1, Pallas kernels: 6.49 us -> 2.36 us  [pack(): pl.pallas_call(pack_kernel, in_specs=[pl.BlockSpec(memory_space=pltpu.SME...]
where the time goes in v6:
time: 130 us
  blocking collectives  85.2 us (66%)
  starting transfers between devices  17.5 us (13%)
  Pallas kernels  12.4 us (10%)
  waiting for transfers between devices  10.5 us (8%)
  local copies, waits for them, and re-layouts  2.29 us (2%)
    all_to_all x5, blocking collectives, swap(): return lax.all_to_all(array, axes, split_axis=0, concat_axis=0, tiled=True)  85.2 us
    all_to_all x2, starting transfers between devices, swap(): return lax.all_to_all(array, axes, split_axis=0, concat_axis=0, tiled=True)  14.4 us
    all_to_all x2, waiting for transfers between devices, swap(): return lax.all_to_all(array, axes, split_axis=0, concat_axis=0, tiled=True)  10.5 us
    pallas_call x1, Pallas kernels, kicks(): pl.pallas_call(kick_kernel, in_specs=[pl.BlockSpec(memory_space=pltpu.SME...  4.93 us
    ppermute x1, starting transfers between devices, local(): lax.ppermute(tail, 'hist', [(i, i + 1) for i in range(hist_size - 1)])  2.82 us
    pallas_call x1, Pallas kernels, deposit(): pl.pallas_call(functools.partial(deposit_kernel, lines, band, parts), in_...  2.75 us
  transfers between devices with their start and end apart: 4, of which 2 were waited for; matrix products, arithmetic and copies ran while one was open for 1% of the time, Pallas kernels for 3%

profile of v6, /device:TPU:1, one launch (start us, length us, event | category | flops | bytes accessed | tf_op | source)
XLA Modules:
  0.0 129.6 jit_solution(13135027073283894635)
XLA Ops:
  0.6 2.4 %pack.1 = (f32[8,4,1024]{2,1,0:T(4,128)}, bf16[2,64,512]{2,1,0:T(8,128)(2,1)}) custom-call(s32[1]{0:T(128)} %bitcast.1.core, s32[4,1024]{1,0:T(4,128)} %row.1, s32[4,1024]{1,0:T(4,128)} %col.1, s32[4,1024]{1,0:T(4,128)} %bins.1, bf16[1024]{0:T(1024)(128)(2,1)} %charge.1, bf16[8,64,512]{2,1,0:T(8,128)(2,1)} %history.3), custom_call_target="tpu_custom_call" | custom-call | tf_op jit(solution)/shard_map/pack/pallas_call | solution.py:72
  3.0 6.5 %all-to-all-start = ((f32[8,4,1024]{2,1,0:T(4,128)}), f32[8,4,1024]{2,1,0:T(4,128)S(1)}, u32[]{:S(2)}, u32[]{:S(2)}) async-start(f32[8,4,1024]{2,1,0:T(4,128)} %get-tuple-element.10), calls=%async_computation | async-start | bytes 262144 | tf_op jit(solution)/shard_map/all_to_all | solution.py:21
  9.5 2.8 %collective-permute-start = (bf16[2,64,512]{2,1,0:T(8,128)(2,1)}, bf16[2,64,512]{2,1,0:T(8,128)(2,1)S(1)}, u32[]{:S(2)}, u32[]{:S(2)}) collective-permute-start(bf16[2,64,512]{2,1,0:T(8,128)(2,1)} %get-tuple-element.11), channel_id=1, source_target_pairs={{0,32},{32,64},{64,96},{96,128},{128,160},{160,192},{192,224},{1,3... | collective-permute-start | bytes 393224 | tf_op jit(solution)/shard_map/ppermute | solution.py:252
  12.4 2.4 %all-to-all-done.particles = f32[8,4,1024]{2,1,0:T(4,128)S(1)} async-done(((f32[8,4,1024]{2,1,0:T(4,128)}), f32[8,4,1024]{2,1,0:T(4,128)S(1)}, u32[]{:S(2)}, u32[]{:S(2)}) %all-to-all-start) | async-done | bytes 131104 | tf_op jit(solution)/shard_map/all_to_all | solution.py:21
  14.8 2.8 %deposit.1 = bf16[32,8,512]{2,1,0:T(8,128)(2,1)S(1)} custom-call(s32[1]{0:T(128)} %bitcast.half, f32[8,4,1024]{2,1,0:T(4,128)S(1)} %all-to-all-done.particles), custom_call_target="tpu_custom_call" | custom-call | flops 4294967296 | bytes 1048576 | tf_op jit(solution)/shard_map/deposit/pallas_call | solution.py:107
  17.6 0.0 copy-start
  17.6 0.0 collective-permute-done.mine
  17.6 20.3 %all_to_all.35 = bf16[32,8,512]{2,1,0:T(8,128)(2,1)S(1)} all-to-all(bf16[32,8,512]{2,1,0:T(8,128)(2,1)S(1)} %deposit.1), channel_id=1, replica_groups=mesh['hist'=8,'xh'=2,'y'=4,'dom'=4] {'y','hist'}, dimensions={0} | all-to-all | bytes 524288 | tf_op jit(solution)/shard_map/all_to_all | solution.py:21
  37.9 0.0 copy-start.1
  37.9 0.1 reduce_sum.39
  38.0 0.7 broadcast_in_dim.6
  38.7 7.8 %all-to-all-start.2 = ((bf16[32,8,512]{2,1,0:T(8,128)(2,1)}), bf16[32,8,512]{2,1,0:T(8,128)(2,1)S(1)}, u32[]{:S(2)}, u32[]{:S(2)}) async-start(bf16[32,8,512]{2,1,0:T(8,128)(2,1)} %broadcast_in_dim.6), calls=%async_computation.2 | async-start | bytes 524288 | tf_op jit(solution)/shard_map/all_to_all | solution.py:21
  46.5 0.3 collective-permute-start.1
  46.9 0.0 copy-done
  46.9 0.0 copy-done.1
  46.9 1.3 old_mixed.1
  48.2 1.5 %copy.11 = bf16[64,8,2,512]{3,1,2,0:T(8,128)(2,1)S(1)} copy(bf16[64,8,2,512]{3,2,1,0:T(2,128)(2,1)} %bitcast.14) | data formatting | bytes 2097152
  49.7 0.0 collective-permute-done.1.other
  49.7 8.0 %all-to-all-done.2.fresh = bf16[32,8,512]{2,1,0:T(8,128)(2,1)S(1)} async-done(((bf16[32,8,512]{2,1,0:T(8,128)(2,1)}), bf16[32,8,512]{2,1,0:T(8,128)(2,1)S(1)}, u32[]{:S(2)}, u32[]{:S(2)}) %all-to-all-start.2) | async-done | bytes 262176 | tf_op jit(solution)/shard_map/all_to_all | solution.py:21
  57.7 1.1 field_parts.1
  58.8 21.6 %all_to_all.36 = bf16[32,16,1024]{2,1,0:T(8,128)(2,1)S(1)} all-to-all(bf16[32,16,1024]{2,1,0:T(8,128)(2,1)S(1)} %get-tuple-element.16), channel_id=1, replica_groups=mesh['hist'=8,'xh'=2,'y'=4,'dom'=4] {'y','dom','xh'}, dimensions={0} | all-to-all | bytes 2097152 | tf_op jit(solution)/shard_map/all_to_all | solution.py:21
  80.4 0.2 convert_reduce_fusion
  80.6 12.9 %all_to_all.37 = f32[8,8,1024]{2,1,0:T(8,128)S(1)} all-to-all(f32[8,8,1024]{2,1,0:T(8,128)S(1)} %bitcast.13), channel_id=1, replica_groups=mesh['hist'=8,'xh'=2,'y'=4,'dom'=4] {'hist'}, dimensions={0} | all-to-all | bytes 524288 | tf_op jit(solution)/shard_map/all_to_all | solution.py:21
  93.4 0.1 broadcast_in_dim.7
  93.5 0.0 copy-start.2
  93.5 15.5 %all_to_all.38 = bf16[32,8,1024]{2,1,0:T(8,128)(2,1)S(1)} all-to-all(bf16[32,8,1024]{2,1,0:T(8,128)(2,1)S(1)} %broadcast_in_dim.7), channel_id=1, replica_groups=mesh['hist'=8,'xh'=2,'y'=4,'dom'=4] {'y','hist'}, dimensions={0} | all-to-all | bytes 1048576 | tf_op jit(solution)/shard_map/all_to_all | solution.py:21
  109.0 4.9 %kicks.1 = f32[8,16,128]{2,1,0:T(8,128)S(1)} custom-call(s32[1]{0:T(128)} %bitcast.half, f32[8,4,1024]{2,1,0:T(4,128)S(1)} %all-to-all-done.particles, bf16[256,1024]{1,0:T(8,128)(2,1)S(1)} %bitcast.11), custom_call_target="tpu_custom_call" | custom-call | tf_op jit(solution)/shard_map/kicks/pallas_call | solution.py:148
  114.0 15.0 %all_to_all.39 = f32[8,16,128]{2,1,0:T(8,128)S(1)} all-to-all(f32[8,16,128]{2,1,0:T(8,128)S(1)} %kicks.1), channel_id=1, replica_groups=mesh['hist'=8,'xh'=2,'y'=4,'dom'=4] {'dom','xh'}, dimensions={0} | all-to-all | bytes 131072 | tf_op jit(solution)/shard_map/all_to_all | solution.py:21
  129.0 0.0 copy-done.2
  129.0 0.6 add.8
  (5 shorter events, 0.1 us)
Async XLA Ops:
  3.0 11.8 %all-to-all-start = ((f32[8,4,1024]{2,1,0:T(4,128)}), f32[8,4,1024]{2,1,0:T(4,128)S(1)}, u32[]{:S(2)}, u32[]{:S(2)}) async-start(f32[8,4,1024]{2,1,0:T(4,128)} %get-tuple-element.10), calls=%async_computation | async-start | bytes 262144 | tf_op jit(solution)/shard_map/all_to_all | solution.py:21
  9.5 8.0 %collective-permute-start = (bf16[2,64,512]{2,1,0:T(8,128)(2,1)}, bf16[2,64,512]{2,1,0:T(8,128)(2,1)S(1)}, u32[]{:S(2)}, u32[]{:S(2)}) collective-permute-start(bf16[2,64,512]{2,1,0:T(8,128)(2,1)} %get-tuple-element.11), channel_id=1, source_target_pairs={{0,32},{32,64},{64,96},{96,128},{128,160},{160,192},{192,224},{1,3... | collective-permute-start | bytes 393224 | tf_op jit(solution)/shard_map/ppermute | solution.py:252
  17.6 29.3 %copy-start = (bf16[8,128,512]{2,1,0:T(8,128)(2,1)S(1)}, bf16[8,128,512]{2,1,0:T(8,128)(2,1)}, u32[]{:S(2)}) copy-start(bf16[8,128,512]{2,1,0:T(8,128)(2,1)} %cols.1) | copy-start | bytes 3145732
  37.9 9.0 %copy-start.1 = (bf16[8,64,512]{2,1,0:T(8,128)(2,1)S(1)}, bf16[8,64,512]{2,1,0:T(8,128)(2,1)}, u32[]{:S(2)}) copy-start(bf16[8,64,512]{2,1,0:T(8,128)(2,1)} %history.3) | copy-start | bytes 1572868
  38.7 19.0 %all-to-all-start.2 = ((bf16[32,8,512]{2,1,0:T(8,128)(2,1)}), bf16[32,8,512]{2,1,0:T(8,128)(2,1)S(1)}, u32[]{:S(2)}, u32[]{:S(2)}) async-start(bf16[32,8,512]{2,1,0:T(8,128)(2,1)} %broadcast_in_dim.6), calls=%async_computation.2 | async-start | bytes 524288 | tf_op jit(solution)/shard_map/all_to_all | solution.py:21
  46.5 3.1 %collective-permute-start.1 = (bf16[2,64,512]{2,1,0:T(8,128)(2,1)S(1)}, bf16[2,64,512]{2,1,0:T(8,128)(2,1)S(1)}, u32[]{:S(2)}, u32[]{:S(2)}) collective-permute-start(bf16[2,64,512]{2,1,0:T(8,128)(2,1)S(1)} %collective-permute-done.mine), channel_id=1, source_target_pairs={{0,1},{1,0},{2,3},{3,2},{4,5},{5,4},{6,7},{7,6},{8,9},{9,8},{10,11... | collective-permute-start | bytes 393224 | tf_op jit(solution)/shard_map/ppermute | solution.py:257
  93.5 35.5 %copy-start.2 = (f32[2,1024]{1,0:T(2,128)S(1)}, f32[2,1024]{1,0:T(2,128)}, u32[]{:S(2)}) copy-start(f32[2,1024]{1,0:T(2,128)} %param.12) | copy-start | bytes 24580
